TPU v7x, 256 devices: a whole 4x4x8 slice. The times are simulated.
256 devices in a mesh: img: 8 (over z_lo, y), space: 32 (over x, z_hi, core).
Axes of the slice: x: 4, y: 4, z: 8 (z_hi: 4, z_lo: 2; z = z_hi * 2 + z_lo), core: 2. Of those that a mesh axis runs over, the one named last changes fastest.
Arguments:
- images: float32 [8, 768, 96, 128], P('img', 'space'), may hold values from -6 to 6
- pairings: int32 [3, 8], replicated, may hold values from 0 to 7, as said below
Outputs:
- advected: float32 [8, 768, 96, 128], P('img', 'space')
- velocity: float32 [8, 3, 768, 96, 128], P('img', None, 'space')
Inputs may be any that keep to these rules, and one draw needn't show every extreme that they name: Each row of pairings is a permutation of the 8 images; an image may be its own partner.
All inputs are finite; a program needn't handle non-finite values.
Results may differ from a plain program's by a relative error of at most 0.00018.
Values sent between devices are 32-bit elements; how exact they have to be, the bound alone decides.
A program may use at most 64 MiB of HBM per device.

v0:
```python
import math

import jax
import jax.numpy as jnp
from jax import lax
from jax.sharding import PartitionSpec as P

RADIUS = 4
PAIRINGS = 3


gauss_sigma = 1.5
step_scale = 8.0
floor_product = 0.25
floor_variance = 0.5


def extended_2(value, sides, width):
    for axis, dim in sides:
        peers, length = (lax.axis_size(axis), value.shape[dim])
        up = [(i, (i + 1) % peers) for i in range(peers - 1)]
        down = [(j, i) for i, j in up]
        last = lax.slice_in_dim(value, length - width, length, axis=dim)
        initial = lax.slice_in_dim(value, 0, width, axis=dim)
        before = lax.ppermute(last, axis, up)
        after = lax.ppermute(initial, axis, down)
        value = jnp.concatenate([before, value, after], axis=dim)
    return value


def gauss_taps(radius):
    raw_taps = [
        math.exp(-(offset * offset) / (2.0 * gauss_sigma * gauss_sigma))
        for offset in range(-radius, radius + 1)
    ]
    total_weight = sum(raw_taps)
    return [raw_weight / total_weight for raw_weight in raw_taps]


def padded_along(volume, dimension, margin):
    widths = [(0, 0)] * volume.ndim
    widths[dimension] = (margin, margin)
    return jnp.pad(volume, widths)


def window(padded, dimension, offset, length):
    return lax.slice_in_dim(padded, offset, offset + length, axis=dimension)


def sum_three(volume, dimension):
    length = volume.shape[dimension]
    padded = padded_along(volume, dimension, 1)
    return (
        window(padded, dimension, 0, length)
        + window(padded, dimension, 1, length)
        + window(padded, dimension, 2, length)
    )


def sum_three_valid(volume, dimension):
    length = volume.shape[dimension] - 2
    return (
        window(volume, dimension, 0, length)
        + window(volume, dimension, 1, length)
        + window(volume, dimension, 2, length)
    )


def box_rows(extended):
    return sum_three(sum_three_valid(extended, 0), 1) / 9.0


def central(volume, dimension):
    length = volume.shape[dimension]
    padded = padded_along(volume, dimension, 1)
    return (window(padded, dimension, 2, length) - window(padded, dimension, 0, length)) * 0.5


def gradient_rows(extended):
    center = extended[1:-1]
    along_rows = (extended[2:] - extended[:-2]) * 0.5
    return jnp.stack([along_rows, central(center, 1), central(center, 2)])


def smooth_along(volume, dimension, weights):
    length = volume.shape[dimension]
    padded = padded_along(volume, dimension, len(weights) // 2)
    result = weights[0] * window(padded, dimension, 0, length)
    for tap_index in range(1, len(weights)):
        result = result + weights[tap_index] * window(padded, dimension, tap_index, length)
    return result


def smooth_rows(extended, weights):
    length = extended.shape[1] - len(weights) + 1
    result = weights[0] * window(extended, 1, 0, length)
    for tap_index in range(1, len(weights)):
        result = result + weights[tap_index] * window(extended, 1, tap_index, length)
    return result


def drive_total(own_extended, partner_extended):
    mean_own = box_rows(own_extended)
    spread_own = box_rows(own_extended * own_extended) - mean_own * mean_own
    center_own = own_extended[1:-1] - mean_own
    guarded_spread = jnp.maximum(spread_own, floor_variance)
    drive_sum = None
    for pairing_row in range(PAIRINGS):
        partner = partner_extended[pairing_row]
        mean_partner = box_rows(partner)
        cross_term = box_rows(own_extended * partner) - mean_own * mean_partner
        spread_partner = box_rows(partner * partner) - mean_partner * mean_partner
        factor = 2.0 * cross_term / jnp.maximum(spread_own * spread_partner, floor_product)
        ratio_term = cross_term / guarded_spread
        pair_term = factor * (partner[1:-1] - mean_partner - ratio_term * center_own)
        drive_sum = pair_term if drive_sum is None else drive_sum + pair_term
    return drive_sum


def advect_rows(near_own, velocity):
    center = near_own[1:-1]
    backward = center - near_own[:-2]
    forward = near_own[2:] - center
    change = jnp.maximum(velocity[0], 0.0) * backward + jnp.minimum(velocity[0], 0.0) * forward
    for dimension in range(1, 3):
        length = center.shape[dimension]
        padded = padded_along(center, dimension, 1)
        backward = center - window(padded, dimension, 0, length)
        forward = window(padded, dimension, 2, length) - center
        speed_part = velocity[dimension]
        change = change + (
            jnp.maximum(speed_part, 0.0) * backward + jnp.minimum(speed_part, 0.0) * forward
        )
    return center - change


def fetch_partners(stacked, pairings):
    pieces = lax.all_to_all(stacked, "img", split_axis=2, concat_axis=0, tiled=True)
    chosen = jnp.take(pieces, pairings, axis=0)
    returned = lax.all_to_all(chosen, "img", split_axis=1, concat_axis=3, tiled=True)
    return returned[:, 0]


def shards(images, pairings):
    weights = gauss_taps(RADIUS)
    own_brick = images[0]
    near_own = extended_2(own_brick, (("space", 0),), 1)
    partners = fetch_partners(images, pairings)
    partner_extended = extended_2(partners, (("space", 1),), 1)
    drive_sum = drive_total(near_own, partner_extended)
    force = drive_sum[None] * gradient_rows(near_own)
    force_extended = extended_2(force, (("space", 1),), RADIUS)
    smoothed = smooth_rows(force_extended, weights)
    smoothed = smooth_along(smoothed, 2, weights)
    smoothed = smooth_along(smoothed, 3, weights)
    velocity = step_scale * smoothed
    advected = advect_rows(near_own, velocity)
    return (advected[None], velocity[None])


def solution(mesh):
    return jax.shard_map(
        shards,
        mesh=mesh,
        in_specs=(P("img", "space", None, None), P()),
        out_specs=(P("img", "space", None, None), P("img", None, "space", None, None)),
        check_vma=False,
    )
```

profile of v0, /device:TPU:29, one launch (start us, length us, event | category | flops | bytes accessed | tf_op | source)
XLA Modules:
  0.0 162.8 jit_solution(5005488709230835332)
XLA Ops:
  0.6 3.0 %copy.9 = f32[1,24,96,128]{3,1,0,2:T(8,128)} copy(f32[1,24,96,128]{3,2,1,0:T(8,128)} %param.2) | data formatting | bytes 2359296 | tf_op args[0]
  3.6 5.6 %all-to-all-start = ((f32[1,24,96,128]{3,1,0,2:T(8,128)}), f32[1,24,96,128]{3,1,0,2:T(8,128)S(1)}, u32[]{:S(2)}, u32[]{:S(2)}) async-start(f32[1,24,96,128]{3,1,0,2:T(8,128)} %copy.9), calls=%async_computation | async-start | bytes 2359296 | tf_op jit(solution)/shard_map/all_to_all | solution.py:138
  9.3 14.1 %all-to-all-done = f32[1,24,96,128]{3,1,0,2:T(8,128)S(1)} async-done(((f32[1,24,96,128]{3,1,0,2:T(8,128)}), f32[1,24,96,128]{3,1,0,2:T(8,128)S(1)}, u32[]{:S(2)}, u32[]{:S(2)}) %all-to-all-start) | async-done | bytes 1179680 | tf_op jit(solution)/shard_map/all_to_all | solution.py:138
  23.4 2.6 %gather_fusion = f32[24,24,12,128]{3,1,2,0:T(8,128)} fusion(f32[8,24,12,128]{3,1,2,0:T(8,128)S(1)} %bitcast.134, s32[1024]{0:T(1024)S(1)} %pad_clamp_fusion), kind=kCustom, calls=%fused_computation | custom fusion | bytes 7077984 | tf_op jit(solution)/shard_map/jit(_take)/gather | solution.py:139
  26.0 2.4 %broadcast_select_fusion = f32[3,8,24,12,128]{4,2,3,1,0:T(8,128)S(1)} fusion(f32[3,8,24,12,128]{4,2,3,1,0:T(8,128)} %bitcast.135, pred[3,8]{1,0:T(4,128)(4,1)S(1)} %compare_and_fusion), kind=kLoop, calls=%fused_computation.75 | loop fusion | flops 884736 | bytes 7077912 | tf_op jit(solution)/shard_map/jit(_take)/select_n | solution.py:139
  28.4 2.0 %copy.10 = f32[3,8,24,12,128]{4,2,3,0,1:T(8,128)} copy(f32[3,8,24,12,128]{4,2,3,1,0:T(8,128)S(1)} %broadcast_select_fusion) | data formatting | bytes 7077888 | tf_op jit(solution)/shard_map/jit(_take)/select_n | solution.py:139
  30.5 6.6 %all-to-all-start.1 = ((f32[3,8,24,12,128]{4,2,3,0,1:T(8,128)}), f32[3,8,24,12,128]{4,2,3,0,1:T(8,128)}, u32[]{:S(2)}, u32[]{:S(2)}) async-start(f32[3,8,24,12,128]{4,2,3,0,1:T(8,128)} %copy.10), calls=%async_computation.1 | async-start | bytes 7077888 | tf_op jit(solution)/shard_map/all_to_all | solution.py:140
  37.1 5.9 %collective-permute-start = (f32[1,96,128]{2,0,1:T(1,128)S(1)}, f32[1,96,128]{2,0,1:T(1,128)S(1)}, u32[]{:S(2)}, u32[]{:S(2)}) collective-permute-start(f32[1,96,128]{2,0,1:T(1,128)S(1)} %bitcast.140), channel_id=1, source_target_pairs={{0,1},{1,2},{2,3},{3,4},{4,5},{5,6},{6,7},{7,8},{8,9},{9,10},{10,1... | collective-permute-start | bytes 147464 | tf_op jit(solution)/shard_map/ppermute | solution.py:25
  43.0 1.9 %collective-permute-start.1 = (f32[1,96,128]{2,0,1:T(1,128)S(1)}, f32[1,96,128]{2,0,1:T(1,128)S(1)}, u32[]{:S(2)}, u32[]{:S(2)}) collective-permute-start(f32[1,96,128]{2,0,1:T(1,128)S(1)} %bitcast.139), channel_id=1, source_target_pairs={{1,0},{2,1},{3,2},{4,3},{5,4},{6,5},{7,6},{8,7},{9,8},{10,9},{11,1... | collective-permute-start | bytes 147464 | tf_op jit(solution)/shard_map/ppermute | solution.py:26
  45.6 30.8 %collective-permute-done = f32[1,96,128]{2,0,1:T(1,128)S(1)} collective-permute-done((f32[1,96,128]{2,0,1:T(1,128)S(1)}, f32[1,96,128]{2,0,1:T(1,128)S(1)}, u32[]{:S(2)}, u32[]{:S(2)}) %collective-permute-start) | collective-permute-done | bytes 49184 | tf_op jit(solution)/shard_map/ppermute | solution.py:25
  76.4 3.2 %fusion.59 = (f32[24,96,128]{2,0,1:T(8,128)}, f32[1,24,96,128]{3,1,2,0:T(8,128)}, f32[1,24,96,128]{3,1,2,0:T(8,128)}, f32[1,24,96,128]{3,1,2,0:T(8,128)}) fusion(f32[1,96,128]{2,0,1:T(1,128)S(1)} %collective-permute-done.1, f32[24,96,128]{2,0,1:T(8,128)S(1)} %bitcast.136, f32[1,96,128]{2,0,1:T(1,128)S(1)} %collective-permute-done), kind=kLoop, calls=%fused_computation.114 | loop fusion | flops 2949120 | bytes 5996544 | tf_op jit(solution)/shard_map/add | solution.py:63
  79.7 2.2 %copy.20 = f32[3,8,24,12,128]{4,2,3,1,0:T(8,128)S(1)} copy(f32[3,8,24,12,128]{4,2,3,0,1:T(8,128)} %all-to-all-done.1) | data formatting | bytes 7077888 | tf_op jit(solution)/shard_map/all_to_all | solution.py:140
  82.1 5.3 %collective-permute-start.2 = (f32[3,1,96,128]{3,1,2,0:T(1,128)S(1)}, f32[3,1,96,128]{3,1,2,0:T(1,128)S(1)}, u32[]{:S(2)}, u32[]{:S(2)}) collective-permute-start(f32[3,1,96,128]{3,1,2,0:T(1,128)S(1)} %get-tuple-element.17), channel_id=1, source_target_pairs={{0,1},{1,2},{2,3},{3,4},{4,5},{5,6},{6,7},{7,8},{8,9},{9,10},{10,1... | collective-permute-start | bytes 442376 | tf_op jit(solution)/shard_map/ppermute | solution.py:25
  87.4 4.8 %collective-permute-start.3 = (f32[3,1,96,128]{3,1,2,0:T(1,128)S(1)}, f32[3,1,96,128]{3,1,2,0:T(1,128)S(1)}, u32[]{:S(2)}, u32[]{:S(2)}) collective-permute-start(f32[3,1,96,128]{3,1,2,0:T(1,128)S(1)} %get-tuple-element.18), channel_id=1, source_target_pairs={{1,0},{2,1},{3,2},{4,3},{5,4},{6,5},{7,6},{8,7},{9,8},{10,9},{11,1... | collective-permute-start | bytes 442376 | tf_op jit(solution)/shard_map/ppermute | solution.py:26
  103.9 5.1 %fusion.76 = f32[24,96,128]{2,0,1:T(8,128)S(1)} fusion(f32[1,1,24,8,12,128]{5,2,4,3,0,1:T(8,128)S(1)} %copy-done.3, f32[1,1,24,8,12,128]{5,2,4,3,0,1:T(8,128)S(1)} %copy-done.2, f32[1,1,24,8,12,128]{5,2,4,3,0,1:T(8,128)S(1)} %get-tuple-element.21, f32[24,96,128]{2,0,1:T(8,128)S(1)} %get-tuple-element.31, f32[24,96,128]{2,0,1:T(8,128)S(1)} %get-tuple-element.14, ...), kind=kLoop, calls=%fused_computation.139 | loop fusion | flops 23003136 | bytes 18874368 | tf_op jit(solution)/shard_map/add | solution.py:116
  110.8 1.9 %collective-permute-start.4 = (f32[3,4,96,128]{3,1,2,0:T(4,128)S(1)}, f32[3,4,96,128]{3,1,2,0:T(4,128)S(1)}, u32[]{:S(2)}, u32[]{:S(2)}) collective-permute-start(f32[3,4,96,128]{3,1,2,0:T(4,128)S(1)} %get-tuple-element.15), channel_id=1, source_target_pairs={{0,1},{1,2},{2,3},{3,4},{4,5},{5,6},{6,7},{7,8},{8,9},{9,10},{10,1... | collective-permute-start | bytes 1769480 | tf_op jit(solution)/shard_map/ppermute | solution.py:25
  112.7 6.9 %collective-permute-start.5 = (f32[3,4,96,128]{3,1,2,0:T(4,128)S(1)}, f32[3,4,96,128]{3,1,2,0:T(4,128)S(1)}, u32[]{:S(2)}, u32[]{:S(2)}) collective-permute-start(f32[3,4,96,128]{3,1,2,0:T(4,128)S(1)} %get-tuple-element.16), channel_id=1, source_target_pairs={{1,0},{2,1},{3,2},{4,3},{5,4},{6,5},{7,6},{8,7},{9,8},{10,9},{11,1... | collective-permute-start | bytes 1769480 | tf_op jit(solution)/shard_map/ppermute | solution.py:26
  119.6 6.3 %collective-permute-done.4 = f32[3,4,96,128]{3,1,2,0:T(4,128)S(1)} collective-permute-done((f32[3,4,96,128]{3,1,2,0:T(4,128)S(1)}, f32[3,4,96,128]{3,1,2,0:T(4,128)S(1)}, u32[]{:S(2)}, u32[]{:S(2)}) %collective-permute-start.4) | collective-permute-done | bytes 589856 | tf_op jit(solution)/shard_map/ppermute | solution.py:25
  125.9 9.2 %collective-permute-done.5 = f32[3,4,96,128]{3,1,2,0:T(4,128)S(1)} collective-permute-done((f32[3,4,96,128]{3,1,2,0:T(4,128)S(1)}, f32[3,4,96,128]{3,1,2,0:T(4,128)S(1)}, u32[]{:S(2)}, u32[]{:S(2)}) %collective-permute-start.5) | collective-permute-done | bytes 589856 | tf_op jit(solution)/shard_map/ppermute | solution.py:26
  135.0 5.1 %fusion.3 = f32[3,24,96,128]{3,1,2,0:T(8,128)S(1)} fusion(f32[3,24,96,128]{3,1,2,0:T(8,128)S(1)} %maximum_multiply_fusion, f32[3,4,96,128]{3,1,2,0:T(4,128)S(1)} %collective-permute-done.5, f32[3,4,96,128]{3,1,2,0:T(4,128)S(1)} %collective-permute-done.4), kind=kLoop, calls=%fused_computation.25 | loop fusion | flops 22118400 | bytes 8257536 | tf_op jit(solution)/shard_map/add | solution.py:98
  140.1 2.6 %multiply_add_fusion = f32[3,24,96,128]{3,1,2,0:T(8,128)S(1)} fusion(f32[3,24,96,128]{3,1,2,0:T(8,128)S(1)} %fusion.3), kind=kLoop, calls=%fused_computation.64 | loop fusion | flops 15040512 | bytes 7077888 | tf_op jit(solution)/shard_map/add | solution.py:90
  142.7 7.5 %fusion.89 = f32[1,3,24,96,128]{4,2,3,1,0:T(8,128)S(1)} fusion(f32[3,24,96,128]{3,1,2,0:T(8,128)S(1)} %multiply_add_fusion), kind=kLoop, calls=%fused_computation.164 | loop fusion | flops 15925248 | bytes 7077888 | tf_op jit(solution)/shard_map/broadcast_in_dim | solution.py:158
  150.2 7.5 %fusion.29 = f32[3,24,96,128]{3,1,2,0:T(8,128)S(1)} fusion(f32[3,24,96,128]{3,1,2,0:T(8,128)S(1)} %multiply_add_fusion), kind=kLoop, calls=%fused_computation.51 | loop fusion | flops 15925248 | bytes 7077888 | tf_op jit(solution)/shard_map/mul | solution.py:156
  157.8 2.4 %copy.13 = f32[1,3,24,96,128]{4,3,2,1,0:T(8,128)} copy(f32[1,3,24,96,128]{4,2,3,1,0:T(8,128)S(1)} %fusion.89) | data formatting | bytes 7077888
  (53 shorter events, 17.0 us)
Async XLA Ops:
  3.6 5.6 %copy-start.14 = (s32[3,8]{1,0:T(4,128)S(1)}, s32[3,8]{1,0:T(4,128)}, u32[]{:S(2)}) copy-start(s32[3,8]{1,0:T(4,128)} %param.3) | copy-start | bytes 292
  3.6 19.8 %all-to-all-start = ((f32[1,24,96,128]{3,1,0,2:T(8,128)}), f32[1,24,96,128]{3,1,0,2:T(8,128)S(1)}, u32[]{:S(2)}, u32[]{:S(2)}) async-start(f32[1,24,96,128]{3,1,0,2:T(8,128)} %copy.9), calls=%async_computation | async-start | bytes 2359296 | tf_op jit(solution)/shard_map/all_to_all | solution.py:138
  30.5 6.6 %copy-start = (f32[1,24,96,128]{3,2,1,0:T(8,128)S(1)}, f32[1,24,96,128]{3,2,1,0:T(8,128)}, u32[]{:S(2)}) copy-start(f32[1,24,96,128]{3,2,1,0:T(8,128)} %param.2) | copy-start | bytes 3538948
  30.5 49.2 %all-to-all-start.1 = ((f32[3,8,24,12,128]{4,2,3,0,1:T(8,128)}), f32[3,8,24,12,128]{4,2,3,0,1:T(8,128)}, u32[]{:S(2)}, u32[]{:S(2)}) async-start(f32[3,8,24,12,128]{4,2,3,0,1:T(8,128)} %copy.10), calls=%async_computation.1 | async-start | bytes 7077888 | tf_op jit(solution)/shard_map/all_to_all | solution.py:140
  37.1 39.3 %collective-permute-start = (f32[1,96,128]{2,0,1:T(1,128)S(1)}, f32[1,96,128]{2,0,1:T(1,128)S(1)}, u32[]{:S(2)}, u32[]{:S(2)}) collective-permute-start(f32[1,96,128]{2,0,1:T(1,128)S(1)} %bitcast.140), channel_id=1, source_target_pairs={{0,1},{1,2},{2,3},{3,4},{4,5},{5,6},{6,7},{7,8},{8,9},{9,10},{10,1... | collective-permute-start | bytes 147464 | tf_op jit(solution)/shard_map/ppermute | solution.py:25
  43.0 33.4 %collective-permute-start.1 = (f32[1,96,128]{2,0,1:T(1,128)S(1)}, f32[1,96,128]{2,0,1:T(1,128)S(1)}, u32[]{:S(2)}, u32[]{:S(2)}) collective-permute-start(f32[1,96,128]{2,0,1:T(1,128)S(1)} %bitcast.139), channel_id=1, source_target_pairs={{1,0},{2,1},{3,2},{4,3},{5,4},{6,5},{7,6},{8,7},{9,8},{10,9},{11,1... | collective-permute-start | bytes 147464 | tf_op jit(solution)/shard_map/ppermute | solution.py:26
  76.4 19.9 %copy-start.10 = (f32[1,96,128]{2,0,1:T(1,128)}, f32[1,96,128]{2,0,1:T(1,128)S(1)}, u32[]{:S(2)}) copy-start(f32[1,96,128]{2,0,1:T(1,128)S(1)} %collective-permute-done) | copy-start | bytes 147460
  76.4 19.9 %copy-start.12 = (f32[1,96,128]{2,0,1:T(1,128)}, f32[1,96,128]{2,0,1:T(1,128)S(1)}, u32[]{:S(2)}) copy-start(f32[1,96,128]{2,0,1:T(1,128)S(1)} %collective-permute-done.1) | copy-start | bytes 147460
  82.1 11.7 %collective-permute-start.2 = (f32[3,1,96,128]{3,1,2,0:T(1,128)S(1)}, f32[3,1,96,128]{3,1,2,0:T(1,128)S(1)}, u32[]{:S(2)}, u32[]{:S(2)}) collective-permute-start(f32[3,1,96,128]{3,1,2,0:T(1,128)S(1)} %get-tuple-element.17), channel_id=1, source_target_pairs={{0,1},{1,2},{2,3},{3,4},{4,5},{5,6},{6,7},{7,8},{8,9},{9,10},{10,1... | collective-permute-start | bytes 442376 | tf_op jit(solution)/shard_map/ppermute | solution.py:25
  87.4 7.4 %collective-permute-start.3 = (f32[3,1,96,128]{3,1,2,0:T(1,128)S(1)}, f32[3,1,96,128]{3,1,2,0:T(1,128)S(1)}, u32[]{:S(2)}, u32[]{:S(2)}) collective-permute-start(f32[3,1,96,128]{3,1,2,0:T(1,128)S(1)} %get-tuple-element.18), channel_id=1, source_target_pairs={{1,0},{2,1},{3,2},{4,3},{5,4},{6,5},{7,6},{8,7},{9,8},{10,9},{11,1... | collective-permute-start | bytes 442376 | tf_op jit(solution)/shard_map/ppermute | solution.py:26
  94.8 0.7 copy-start.8
  100.2 1.3 copy-start.2
  100.3 1.6 copy-start.3
  100.3 1.6 copy-start.9
  101.9 1.3 copy-start.1
  101.9 1.6 copy-start.4
  101.9 2.0 %copy-start.5 = (f32[24,96,128]{2,0,1:T(8,128)S(1)}, f32[24,96,128]{2,0,1:T(8,128)}, u32[]{:S(2)}) copy-start(f32[24,96,128]{2,0,1:T(8,128)} %slice_add_fusion.12) | copy-start | bytes 3538948
  103.9 5.2 %copy-start.6 = (f32[1,24,96,128]{3,1,2,0:T(8,128)S(1)}, f32[1,24,96,128]{3,1,2,0:T(8,128)}, u32[]{:S(2)}) copy-start(f32[1,24,96,128]{3,1,2,0:T(8,128)} %get-tuple-element.26) | copy-start | bytes 3538948
  103.9 5.2 %copy-start.7 = (f32[1,24,96,128]{3,1,2,0:T(8,128)S(1)}, f32[1,24,96,128]{3,1,2,0:T(8,128)}, u32[]{:S(2)}) copy-start(f32[1,24,96,128]{3,1,2,0:T(8,128)} %get-tuple-element.27) | copy-start | bytes 3538948
  110.8 15.1 %collective-permute-start.4 = (f32[3,4,96,128]{3,1,2,0:T(4,128)S(1)}, f32[3,4,96,128]{3,1,2,0:T(4,128)S(1)}, u32[]{:S(2)}, u32[]{:S(2)}) collective-permute-start(f32[3,4,96,128]{3,1,2,0:T(4,128)S(1)} %get-tuple-element.15), channel_id=1, source_target_pairs={{0,1},{1,2},{2,3},{3,4},{4,5},{5,6},{6,7},{7,8},{8,9},{9,10},{10,1... | collective-permute-start | bytes 1769480 | tf_op jit(solution)/shard_map/ppermute | solution.py:25
  112.7 22.3 %collective-permute-start.5 = (f32[3,4,96,128]{3,1,2,0:T(4,128)S(1)}, f32[3,4,96,128]{3,1,2,0:T(4,128)S(1)}, u32[]{:S(2)}, u32[]{:S(2)}) collective-permute-start(f32[3,4,96,128]{3,1,2,0:T(4,128)S(1)} %get-tuple-element.16), channel_id=1, source_target_pairs={{1,0},{2,1},{3,2},{4,3},{5,4},{6,5},{7,6},{8,7},{9,8},{10,9},{11,1... | collective-permute-start | bytes 1769480 | tf_op jit(solution)/shard_map/ppermute | solution.py:26
  157.8 2.4 %copy-start.11 = (f32[1,96,128]{2,0,1:T(1,128)S(1)}, f32[1,96,128]{2,0,1:T(1,128)}, u32[]{:S(2)}) copy-start(f32[1,96,128]{2,0,1:T(1,128)} %copy-done.10) | copy-start | bytes 147460
  157.8 2.4 %copy-start.13 = (f32[1,96,128]{2,0,1:T(1,128)S(1)}, f32[1,96,128]{2,0,1:T(1,128)}, u32[]{:S(2)}) copy-start(f32[1,96,128]{2,0,1:T(1,128)} %copy-done.12) | copy-start | bytes 147460
where the time goes:
time: 164 us; the launch traced here: 163 us
  waiting for transfers between devices  61.4 us (37%)
  other arithmetic  42.8 us (26%)
  starting transfers between devices  38.9 us (24%)
  local copies, waits for them, and re-layouts  19 us (12%)
    ppermute x3, waiting for transfers between devices, extended_2(): before = lax.ppermute(last, axis, up)  37.1 us
    all_to_all x1, waiting for transfers between devices, fetch_partners(): lax.all_to_all(stacked, 'img', split_axis=2, concat_axis=0, tiled=True)  14.1 us
    ppermute x3, starting transfers between devices, extended_2(): after = lax.ppermute(initial, axis, down)  13.5 us
    ppermute x3, starting transfers between devices, extended_2(): before = lax.ppermute(last, axis, up)  13.1 us
    ppermute x3, waiting for transfers between devices, extended_2(): after = lax.ppermute(initial, axis, down)  10.1 us
    unnamed x34, local copies, waits for them, and re-layouts  9.96 us
    broadcast_in_dim x2, other arithmetic, shards(): return (advected[None], velocity[None])  8.92 us
    mul x1, other arithmetic, shards(): velocity = step_scale * smoothed  7.53 us
  transfers between devices with their start and end apart: 8, of which 5 were waited for; matrix products, arithmetic and copies ran while one was open for 3% of the time, Pallas kernels for 0%

commit v1 on v0

v1 whole, which is shorter than its diff:
```python
import math

import jax
import jax.numpy as jnp
from jax import lax
from jax.sharding import PartitionSpec as P

RADIUS = 4
PAIRINGS = 3

gauss_sigma = 1.5
step_scale = 8.0
floor_product = 0.25
floor_variance = 0.5

Y_MARGIN = 2


def gauss_taps(radius):
    raw_taps = [
        math.exp(-(offset * offset) / (2.0 * gauss_sigma * gauss_sigma))
        for offset in range(-radius, radius + 1)
    ]
    total_weight = sum(raw_taps)
    return [raw_weight / total_weight for raw_weight in raw_taps]


def halo_rows(value, width):
    peers = lax.axis_size("space")
    up = [(i, i + 1) for i in range(peers - 1)]
    down = [(i + 1, i) for i in range(peers - 1)]
    before = lax.ppermute(value[-width:], "space", up)
    after = lax.ppermute(value[:width], "space", down)
    return jnp.concatenate([before, value, after], axis=0)


def padded_along(volume, dimension, margin):
    widths = [(0, 0)] * volume.ndim
    widths[dimension] = (margin, margin)
    return jnp.pad(volume, widths)


def window(padded, dimension, offset, length):
    return lax.slice_in_dim(padded, offset, offset + length, axis=dimension)


def central(volume, dimension):
    length = volume.shape[dimension]
    padded = padded_along(volume, dimension, 1)
    return (window(padded, dimension, 2, length) - window(padded, dimension, 0, length)) * 0.5


def smooth_along(volume, dimension, weights):
    length = volume.shape[dimension]
    padded = padded_along(volume, dimension, len(weights) // 2)
    result = weights[0] * window(padded, dimension, 0, length)
    for tap_index in range(1, len(weights)):
        result = result + weights[tap_index] * window(padded, dimension, tap_index, length)
    return result


def smooth_rows(extended, weights):
    length = extended.shape[1] - len(weights) + 1
    result = weights[0] * window(extended, 1, 0, length)
    for tap_index in range(1, len(weights)):
        result = result + weights[tap_index] * window(extended, 1, tap_index, length)
    return result


def box_valid(volume):
    sx = volume[..., :-2, :, :] + volume[..., 1:-1, :, :] + volume[..., 2:, :, :]
    sy = sx[..., :-2, :] + sx[..., 1:-1, :] + sx[..., 2:, :]
    return sy / 9.0


def slice_drive(stack, pairings, rows):
    keep = slice(Y_MARGIN - 1, Y_MARGIN - 1 + rows)
    center = stack[:, 1:-1, Y_MARGIN:Y_MARGIN + rows]
    mean = box_valid(stack)[:, :, keep]
    spread = box_valid(stack * stack)[:, :, keep] - mean * mean
    guarded_spread = jnp.maximum(spread, floor_variance)
    centered = center - mean
    drive_sum = None
    for pairing_row in range(PAIRINGS):
        index = pairings[pairing_row]
        partner = jnp.take(stack, index, axis=0)
        mean_partner = jnp.take(mean, index, axis=0)
        spread_partner = jnp.take(spread, index, axis=0)
        partner_center = jnp.take(center, index, axis=0)
        cross_term = box_valid(stack * partner)[:, :, keep] - mean * mean_partner
        factor = 2.0 * cross_term / jnp.maximum(spread * spread_partner, floor_product)
        ratio_term = cross_term / guarded_spread
        pair_term = factor * (partner_center - mean_partner - ratio_term * centered)
        drive_sum = pair_term if drive_sum is None else drive_sum + pair_term
    return drive_sum


def advect_rows(near_own, velocity):
    center = near_own[1:-1]
    backward = center - near_own[:-2]
    forward = near_own[2:] - center
    change = jnp.maximum(velocity[0], 0.0) * backward + jnp.minimum(velocity[0], 0.0) * forward
    for dimension in range(1, 3):
        length = center.shape[dimension]
        padded = padded_along(center, dimension, 1)
        backward = center - window(padded, dimension, 0, length)
        forward = window(padded, dimension, 2, length) - center
        speed_part = velocity[dimension]
        change = change + (
            jnp.maximum(speed_part, 0.0) * backward + jnp.minimum(speed_part, 0.0) * forward
        )
    return center - change


def shards(images, pairings):
    weights = gauss_taps(RADIUS)
    groups = lax.axis_size("img")
    own = images[0]
    x_rows, y_rows, _ = own.shape
    rows = y_rows // groups
    own_ext = halo_rows(own, RADIUS + 1)
    near = own_ext[RADIUS:-RADIUS]
    padded = jnp.pad(near, ((0, 0), (Y_MARGIN, Y_MARGIN), (0, 0)))
    width = rows + 2 * Y_MARGIN
    pieces = jnp.stack([padded[:, j * rows:j * rows + width] for j in range(groups)])
    stack = lax.all_to_all(pieces, "img", split_axis=0, concat_axis=0, tiled=True)
    drive_part = slice_drive(stack, pairings, rows)
    drive_sum = lax.all_to_all(drive_part, "img", split_axis=0, concat_axis=2, tiled=True)[0]
    drive_ext = halo_rows(drive_sum, RADIUS)
    center = own_ext[1:-1]
    gradient = jnp.stack(
        [(own_ext[2:] - own_ext[:-2]) * 0.5, central(center, 1), central(center, 2)]
    )
    force = drive_ext[None] * gradient
    smoothed = smooth_rows(force, weights)
    smoothed = smooth_along(smoothed, 2, weights)
    smoothed = smooth_along(smoothed, 3, weights)
    velocity = step_scale * smoothed
    advected = advect_rows(near, velocity)
    return (advected[None], velocity[None])


def solution(mesh):
    return jax.shard_map(
        shards,
        mesh=mesh,
        in_specs=(P("img", "space", None, None), P()),
        out_specs=(P("img", "space", None, None), P("img", None, "space", None, None)),
        check_vma=False,
    )
```

time: 164 us -> 181 us (1.10)
  the two profiles are of different devices: /device:TPU:29 before, /device:TPU:6 now
where the time goes in v1:
time: 181 us; the launch traced here: 180 us
  local copies, waits for them, and re-layouts  51.7 us (29%)
  other arithmetic  49.5 us (27%)
  waiting for transfers between devices  36.1 us (20%)
  blocking collectives  20.9 us (12%)
  starting transfers between devices  20.8 us (11%)
    all_to_all x1, waiting for transfers between devices, shards(): lax.all_to_all(pieces, 'img', split_axis=0, concat_axis=0, tiled=True)  22.2 us
    all_to_all x1, blocking collectives, shards(): lax.all_to_all(drive_part, 'img', split_axis=0, concat_axis=2, tiled=True)  20.9 us
    ppermute x2, starting transfers between devices, halo_rows(): after = lax.ppermute(value[:width], 'space', down)  12.1 us
    broadcast_in_dim x2, other arithmetic, shards(): return (advected[None], velocity[None])  11.3 us
    ppermute x2, waiting for transfers between devices, halo_rows(): before = lax.ppermute(value[-width:], 'space', up)  10 us
    gather x3, local copies, waits for them, and re-layouts, slice_drive(): spread_partner = jnp.take(spread, index, axis=0)  9.73 us
    gather x3, local copies, waits for them, and re-layouts, slice_drive(): partner_center = jnp.take(center, index, axis=0)  9.68 us
    gather x3, local copies, waits for them, and re-layouts, slice_drive(): mean_partner = jnp.take(mean, index, axis=0)  9.64 us
  transfers between devices with their start and end apart: 5, of which 5 were waited for; matrix products, arithmetic and copies ran while one was open for 1% of the time, Pallas kernels for 0%

profile of v1, /device:TPU:6, one launch (start us, length us, event | category | flops | bytes accessed | tf_op | source)
XLA Modules:
  0.0 179.9 jit_solution(13760686319762841480)
XLA Ops:
  3.7 7.9 %collective-permute-start.1 = (f32[5,96,128]{2,1,0:T(8,128)S(1)}, f32[5,96,128]{2,1,0:T(8,128)S(1)}, u32[]{:S(2)}, u32[]{:S(2)}) collective-permute-start(f32[5,96,128]{2,1,0:T(8,128)S(1)} %get-tuple-element.40), channel_id=1, source_target_pairs={{1,0},{2,1},{3,2},{4,3},{5,4},{6,5},{7,6},{8,7},{9,8},{10,9},{11,1... | collective-permute-start | bytes 737288 | tf_op jit(solution)/shard_map/ppermute | solution.py:33
  14.1 3.8 %collective-permute-done.1 = f32[5,96,128]{2,1,0:T(8,128)S(1)} collective-permute-done((f32[5,96,128]{2,1,0:T(8,128)S(1)}, f32[5,96,128]{2,1,0:T(8,128)S(1)}, u32[]{:S(2)}, u32[]{:S(2)}) %collective-permute-start.1) | collective-permute-done | bytes 245792 | tf_op jit(solution)/shard_map/ppermute | solution.py:33
  25.7 4.6 %all-to-all-start = ((f32[8,26,16,128]{3,2,1,0:T(8,128)}), f32[8,26,16,128]{3,2,1,0:T(8,128)S(1)}, u32[]{:S(2)}, u32[]{:S(2)}) async-start(f32[8,26,16,128]{3,2,1,0:T(8,128)} %fusion.84), calls=%async_computation | async-start | bytes 3407872 | tf_op jit(solution)/shard_map/all_to_all | solution.py:126
  30.4 22.2 %all-to-all-done = f32[8,26,16,128]{3,2,1,0:T(8,128)S(1)} async-done(((f32[8,26,16,128]{3,2,1,0:T(8,128)}), f32[8,26,16,128]{3,2,1,0:T(8,128)S(1)}, u32[]{:S(2)}, u32[]{:S(2)}) %all-to-all-start) | async-done | bytes 1703968 | tf_op jit(solution)/shard_map/all_to_all | solution.py:126
  53.8 3.3 %gather_fusion.7 = f32[8,24,12,128]{3,2,1,0:T(8,128)} fusion(f32[8,24,12,128]{3,2,1,0:T(8,128)} %slice.467, s32[1024]{0:T(1024)S(1)} %get-tuple-element.46), kind=kCustom, calls=%fused_computation.8.clone | custom fusion | bytes 2359328 | tf_op jit(solution)/shard_map/jit(_take)/gather | solution.py:89
  57.1 3.2 %gather_fusion.11 = f32[8,24,12,128]{3,2,1,0:T(8,128)} fusion(f32[8,24,12,128]{3,2,1,0:T(8,128)} %slice.467, s32[1024]{0:T(1024)S(1)} %get-tuple-element.45), kind=kCustom, calls=%fused_computation.11.clone | custom fusion | bytes 2359328 | tf_op jit(solution)/shard_map/jit(_take)/gather | solution.py:89
  60.3 3.2 %gather_fusion.3 = f32[8,24,12,128]{3,2,1,0:T(8,128)} fusion(f32[8,24,12,128]{3,2,1,0:T(8,128)} %slice.467, s32[1024]{0:T(1024)S(1)} %pad_clamp_fusion.2), kind=kCustom, calls=%fused_computation.5.clone | custom fusion | bytes 2359328 | tf_op jit(solution)/shard_map/jit(_take)/gather | solution.py:89
  69.1 5.1 %select_multiply_fusion.2 = (f32[8,26,16,128]{3,2,1,0:T(8,128)}, f32[8,26,16,128]{3,2,1,0:T(8,128)S(1)}, f32[8,26,16,128]{3,2,1,0:T(8,128)}, f32[8,26,16,128]{3,2,1,0:T(8,128)}) fusion(f32[8,26,16,128]{3,2,1,0:T(8,128)S(1)} %all-to-all-done, f32[8,26,16,128]{3,2,1,0:T(8,128)} %gather_fusion, pred[8]{0:T(512)(128)(4,1)S(1)} %get-tuple-element.6, ...), kind=kLoop, calls=%fused_computation.70 | loop fusion | flops 2981888 | bytes 13631512 | tf_op jit(solution)/shard_map/mul | solution.py:90
  75.4 2.7 %fusion.43 = (f32[8,24,12,128]{3,2,1,0:T(8,128)}, f32[8,24,12,128]{3,2,1,0:T(8,128)}) fusion(f32[8,24,14,128]{3,2,1,0:T(8,128)S(1)} %get-tuple-element.33, f32[8,24,14,128]{3,2,1,0:T(8,128)S(1)} %get-tuple-element.34, f32[8,24,14,128]{3,2,1,0:T(8,128)S(1)} %get-tuple-element.32, f32[8,24,14,128]{3,2,1,0:T(8,128)S(1)} %get-tuple-element.30, ...), kind=kLoop, calls=%fused_computation.97 | loop fusion | flops 2359296 | bytes 9437184 | tf_op jit(solution)/shard_map/sub | solution.py:80
  78.2 3.2 %gather_fusion.6 = f32[8,24,12,128]{3,2,1,0:T(8,128)} fusion(f32[8,24,12,128]{3,2,1,0:T(8,128)} %get-tuple-element.12, s32[1024]{0:T(1024)S(1)} %get-tuple-element.46), kind=kCustom, calls=%fused_computation.7.clone | custom fusion | bytes 2359328 | tf_op jit(solution)/shard_map/jit(_take)/gather | solution.py:88
  81.4 3.3 %gather_fusion.10 = f32[8,24,12,128]{3,2,1,0:T(8,128)} fusion(f32[8,24,12,128]{3,2,1,0:T(8,128)} %get-tuple-element.12, s32[1024]{0:T(1024)S(1)} %get-tuple-element.45), kind=kCustom, calls=%fused_computation.10.clone | custom fusion | bytes 2359328 | tf_op jit(solution)/shard_map/jit(_take)/gather | solution.py:88
  84.6 3.2 %gather_fusion.5 = f32[8,24,12,128]{3,2,1,0:T(8,128)} fusion(f32[8,24,12,128]{3,2,1,0:T(8,128)} %get-tuple-element.13, s32[1024]{0:T(1024)S(1)} %get-tuple-element.46), kind=kCustom, calls=%fused_computation.6.clone | custom fusion | bytes 2359328 | tf_op jit(solution)/shard_map/jit(_take)/gather | solution.py:87
  87.8 3.2 %gather_fusion.9 = f32[8,24,12,128]{3,2,1,0:T(8,128)} fusion(f32[8,24,12,128]{3,2,1,0:T(8,128)} %get-tuple-element.13, s32[1024]{0:T(1024)S(1)} %get-tuple-element.45), kind=kCustom, calls=%fused_computation.9.clone | custom fusion | bytes 2359328 | tf_op jit(solution)/shard_map/jit(_take)/gather | solution.py:87
  91.1 3.3 %gather_fusion.2 = f32[8,24,12,128]{3,2,1,0:T(8,128)} fusion(f32[8,24,12,128]{3,2,1,0:T(8,128)} %get-tuple-element.12, s32[1024]{0:T(1024)S(1)} %pad_clamp_fusion.2), kind=kCustom, calls=%fused_computation.4.clone | custom fusion | bytes 2359328 | tf_op jit(solution)/shard_map/jit(_take)/gather | solution.py:88
  94.3 3.2 %gather_fusion.1 = f32[8,24,12,128]{3,2,1,0:T(8,128)} fusion(f32[8,24,12,128]{3,2,1,0:T(8,128)} %get-tuple-element.13, s32[1024]{0:T(1024)S(1)} %pad_clamp_fusion.2), kind=kCustom, calls=%fused_computation.1.clone | custom fusion | bytes 2359328 | tf_op jit(solution)/shard_map/jit(_take)/gather | solution.py:87
  97.5 2.8 %slice_add_fusion.18 = f32[8,24,16,128]{3,2,1,0:T(8,128)S(1)} fusion(f32[8,26,16,128]{3,2,1,0:T(8,128)} %get-tuple-element.14), kind=kLoop, calls=%fused_computation.110 | loop fusion | flops 786432 | bytes 6291456 | tf_op jit(solution)/shard_map/add | solution.py:71
  105.3 8.1 %fusion.49 = f32[8,24,12,128]{3,2,1,0:T(8,128)} fusion(f32[8,24,12,128]{3,2,1,0:T(8,128)} %gather_fusion.11, f32[8,24,12,128]{3,2,1,0:T(8,128)S(1)} %copy-done, f32[8,24,12,128]{3,2,1,0:T(8,128)} %gather_fusion.10, f32[8,24,12,128]{3,2,1,0:T(8,128)S(1)} %copy-done.5, f32[8,24,12,128]{3,2,1,0:T(8,128)} %gather_fusion.6, f32[8,24,12,128]{3,2,1,0:T(8,128)} %gather_fusion.3, ...), kind=kLoop, calls=%fused_computation.116 | loop fusion | flops 16220160 | bytes 25952280 | tf_op jit(solution)/shard_map/add | solution.py:94
  115.2 20.9 %all_to_all.20 = f32[8,24,12,128]{3,1,2,0:T(8,128)S(1)} all-to-all(f32[8,24,12,128]{3,1,2,0:T(8,128)S(1)} %copy.23), channel_id=1, replica_groups=mesh['img'=8,'space'=32] {'img'}, dimensions={0} | all-to-all | bytes 2359296 | tf_op jit(solution)/shard_map/all_to_all | solution.py:128
  136.1 4.2 %collective-permute-start.3 = (f32[4,96,128]{2,0,1:T(4,128)S(1)}, f32[4,96,128]{2,0,1:T(4,128)S(1)}, u32[]{:S(2)}, u32[]{:S(2)}) collective-permute-start(f32[4,96,128]{2,0,1:T(4,128)S(1)} %bitcast.80), channel_id=1, source_target_pairs={{1,0},{2,1},{3,2},{4,3},{5,4},{6,5},{7,6},{8,7},{9,8},{10,9},{11,1... | collective-permute-start | bytes 589832 | tf_op jit(solution)/shard_map/ppermute | solution.py:33
  144.0 7.5 %collective-permute-done.2 = f32[4,96,128]{2,0,1:T(4,128)S(1)} collective-permute-done((f32[4,96,128]{2,0,1:T(4,128)S(1)}, f32[4,96,128]{2,0,1:T(4,128)S(1)}, u32[]{:S(2)}, u32[]{:S(2)}) %collective-permute-start.2) | collective-permute-done | bytes 196640 | tf_op jit(solution)/shard_map/ppermute | solution.py:32
  153.3 3.9 %fusion.17 = f32[3,24,96,128]{3,2,1,0:T(8,128)S(1)} fusion(f32[3,32,96,128]{3,2,1,0:T(8,128)S(1)} %maximum_multiply_fusion), kind=kLoop, calls=%fused_computation.41 | loop fusion | flops 15040512 | bytes 35389440 | tf_op jit(solution)/shard_map/add | solution.py:66
  157.2 3.8 %multiply_add_fusion = f32[3,24,96,128]{3,2,1,0:T(8,128)S(1)} fusion(f32[3,24,96,128]{3,2,1,0:T(8,128)S(1)} %fusion.17), kind=kLoop, calls=%fused_computation.57 | loop fusion | flops 15040512 | bytes 7077888 | tf_op jit(solution)/shard_map/add | solution.py:58
  161.0 8.7 %fusion.98 = f32[1,3,24,96,128]{4,3,2,1,0:T(8,128)} fusion(f32[3,24,96,128]{3,2,1,0:T(8,128)S(1)} %multiply_add_fusion), kind=kLoop, calls=%fused_computation.193 | loop fusion | flops 15925248 | bytes 7077888 | tf_op jit(solution)/shard_map/broadcast_in_dim | solution.py:140
  169.7 7.5 %fusion.9 = f32[3,24,96,128]{3,2,1,0:T(8,128)S(1)} fusion(f32[3,24,96,128]{3,2,1,0:T(8,128)S(1)} %multiply_add_fusion), kind=kLoop, calls=%fused_computation.32 | loop fusion | flops 15925248 | bytes 7077888 | tf_op jit(solution)/shard_map/mul | solution.py:138
  (61 shorter events, 36.3 us)
Async XLA Ops:
  1.7 12.4 %collective-permute-start = (f32[5,96,128]{2,1,0:T(8,128)S(1)}, f32[5,96,128]{2,1,0:T(8,128)S(1)}, u32[]{:S(2)}, u32[]{:S(2)}) collective-permute-start(f32[5,96,128]{2,1,0:T(8,128)S(1)} %get-tuple-element.39), channel_id=1, source_target_pairs={{0,1},{1,2},{2,3},{3,4},{4,5},{5,6},{6,7},{7,8},{8,9},{9,10},{10,1... | collective-permute-start | bytes 737288 | tf_op jit(solution)/shard_map/ppermute | solution.py:32
  3.7 14.2 %collective-permute-start.1 = (f32[5,96,128]{2,1,0:T(8,128)S(1)}, f32[5,96,128]{2,1,0:T(8,128)S(1)}, u32[]{:S(2)}, u32[]{:S(2)}) collective-permute-start(f32[5,96,128]{2,1,0:T(8,128)S(1)} %get-tuple-element.40), channel_id=1, source_target_pairs={{1,0},{2,1},{3,2},{4,3},{5,4},{6,5},{7,6},{8,7},{9,8},{10,9},{11,1... | collective-permute-start | bytes 737288 | tf_op jit(solution)/shard_map/ppermute | solution.py:33
  14.1 3.8 %copy-start.6 = (f32[5,96,128]{2,1,0:T(8,128)}, f32[5,96,128]{2,1,0:T(8,128)S(1)}, u32[]{:S(2)}) copy-start(f32[5,96,128]{2,1,0:T(8,128)S(1)} %collective-permute-done) | copy-start | bytes 737284
  17.9 0.7 copy-start.8
  25.7 4.6 %copy-start.10 = (s32[3,8]{1,0:T(4,128)S(1)}, s32[3,8]{1,0:T(4,128)}, u32[]{:S(2)}) copy-start(s32[3,8]{1,0:T(4,128)} %param.7) | copy-start | bytes 292
  25.7 26.8 %all-to-all-start = ((f32[8,26,16,128]{3,2,1,0:T(8,128)}), f32[8,26,16,128]{3,2,1,0:T(8,128)S(1)}, u32[]{:S(2)}, u32[]{:S(2)}) async-start(f32[8,26,16,128]{3,2,1,0:T(8,128)} %fusion.84), calls=%async_computation | async-start | bytes 3407872 | tf_op jit(solution)/shard_map/all_to_all | solution.py:126
  97.5 2.9 %copy-start.3 = (f32[8,26,16,128]{3,2,1,0:T(8,128)S(1)}, f32[8,26,16,128]{3,2,1,0:T(8,128)}, u32[]{:S(2)}) copy-start(f32[8,26,16,128]{3,2,1,0:T(8,128)} %get-tuple-element.16) | copy-start | bytes 5111812
  100.4 1.5 copy-start.2
  102.9 1.4 copy-start
  103.0 1.9 %copy-start.1 = (f32[8,24,12,128]{3,2,1,0:T(8,128)S(1)}, f32[8,24,12,128]{3,2,1,0:T(8,128)}, u32[]{:S(2)}) copy-start(f32[8,24,12,128]{3,2,1,0:T(8,128)} %get-tuple-element.13) | copy-start | bytes 3538948
  103.0 2.3 %copy-start.5 = (f32[8,24,12,128]{3,2,1,0:T(8,128)S(1)}, f32[8,24,12,128]{3,2,1,0:T(8,128)}, u32[]{:S(2)}) copy-start(f32[8,24,12,128]{3,2,1,0:T(8,128)} %gather_fusion.7) | copy-start | bytes 3538948
  136.1 8.0 %collective-permute-start.3 = (f32[4,96,128]{2,0,1:T(4,128)S(1)}, f32[4,96,128]{2,0,1:T(4,128)S(1)}, u32[]{:S(2)}, u32[]{:S(2)}) collective-permute-start(f32[4,96,128]{2,0,1:T(4,128)S(1)} %bitcast.80), channel_id=1, source_target_pairs={{1,0},{2,1},{3,2},{4,3},{5,4},{6,5},{7,6},{8,7},{9,8},{10,9},{11,1... | collective-permute-start | bytes 589832 | tf_op jit(solution)/shard_map/ppermute | solution.py:33
  140.3 11.2 %collective-permute-start.2 = (f32[4,96,128]{2,0,1:T(4,128)S(1)}, f32[4,96,128]{2,0,1:T(4,128)S(1)}, u32[]{:S(2)}, u32[]{:S(2)}) collective-permute-start(f32[4,96,128]{2,0,1:T(4,128)S(1)} %bitcast.79), channel_id=1, source_target_pairs={{0,1},{1,2},{2,3},{3,4},{4,5},{5,6},{6,7},{7,8},{8,9},{9,10},{10,1... | collective-permute-start | bytes 589832 | tf_op jit(solution)/shard_map/ppermute | solution.py:32
  169.7 7.5 %copy-start.4 = (f32[1,24,96,128]{3,2,1,0:T(8,128)S(1)}, f32[1,24,96,128]{3,2,1,0:T(8,128)}, u32[]{:S(2)}) copy-start(f32[1,24,96,128]{3,2,1,0:T(8,128)} %param.6) | copy-start | bytes 3538948
  169.7 7.5 %copy-start.7 = (f32[5,96,128]{2,1,0:T(8,128)S(1)}, f32[5,96,128]{2,1,0:T(8,128)}, u32[]{:S(2)}) copy-start(f32[5,96,128]{2,1,0:T(8,128)} %copy-done.6) | copy-start | bytes 737284
  169.7 7.5 %copy-start.9 = (f32[5,96,128]{2,1,0:T(8,128)S(1)}, f32[5,96,128]{2,1,0:T(8,128)}, u32[]{:S(2)}) copy-start(f32[5,96,128]{2,1,0:T(8,128)} %copy-done.8) | copy-start | bytes 737284

commit v2 on v1

--- a/solution.py
+++ b/solution.py
@@ -3,6 +3,8 @@
 import jax
 import jax.numpy as jnp
 from jax import lax
+from jax.experimental import pallas as pl
+from jax.experimental.pallas import tpu as pltpu
 from jax.sharding import PartitionSpec as P
 
 RADIUS = 4
@@ -12,8 +14,6 @@
 step_scale = 8.0
 floor_product = 0.25
 floor_variance = 0.5
-
-Y_MARGIN = 2
 
 
 def gauss_taps(radius):
@@ -67,32 +67,63 @@
     return result
 
 
-def box_valid(volume):
-    sx = volume[..., :-2, :, :] + volume[..., 1:-1, :, :] + volume[..., 2:, :, :]
-    sy = sx[..., :-2, :] + sx[..., 1:-1, :] + sx[..., 2:, :]
-    return sy / 9.0
+def box_rows(volume):
+    sx = volume[:-2] + volume[1:-1] + volume[2:]
+    last = sx.shape[1] - 1
+    row = lax.broadcasted_iota(jnp.int32, sx.shape, 1)
+    before = jnp.where(row >= 1, pltpu.roll(sx, 1, 1), 0.0)
+    after = jnp.where(row < last, pltpu.roll(sx, last, 1), 0.0)
+    return (before + sx + after) / 9.0
 
 
-def slice_drive(stack, pairings, rows):
-    keep = slice(Y_MARGIN - 1, Y_MARGIN - 1 + rows)
-    center = stack[:, 1:-1, Y_MARGIN:Y_MARGIN + rows]
-    mean = box_valid(stack)[:, :, keep]
-    spread = box_valid(stack * stack)[:, :, keep] - mean * mean
-    guarded_spread = jnp.maximum(spread, floor_variance)
-    centered = center - mean
-    drive_sum = None
-    for pairing_row in range(PAIRINGS):
-        index = pairings[pairing_row]
-        partner = jnp.take(stack, index, axis=0)
-        mean_partner = jnp.take(mean, index, axis=0)
-        spread_partner = jnp.take(spread, index, axis=0)
-        partner_center = jnp.take(center, index, axis=0)
-        cross_term = box_valid(stack * partner)[:, :, keep] - mean * mean_partner
-        factor = 2.0 * cross_term / jnp.maximum(spread * spread_partner, floor_product)
-        ratio_term = cross_term / guarded_spread
-        pair_term = factor * (partner_center - mean_partner - ratio_term * centered)
-        drive_sum = pair_term if drive_sum is None else drive_sum + pair_term
-    return drive_sum
+def drive_kernel(pair_ref, stack_ref, out_ref, mean_ref, spread_ref):
+    groups = stack_ref.shape[0]
+
+    def stats(g, carry):
+        value = stack_ref[g]
+        mean = box_rows(value)
+        mean_ref[g] = mean
+        spread_ref[g] = box_rows(value * value) - mean * mean
+        return carry
+
+    lax.fori_loop(0, groups, stats, 0)
+
+    def pairs(g, carry):
+        own = stack_ref[g]
+        mean_own = mean_ref[g]
+        spread_own = spread_ref[g]
+        center_own = own[1:-1] - mean_own
+        guarded_spread = jnp.maximum(spread_own, floor_variance)
+        drive_sum = None
+        for pairing_row in range(PAIRINGS):
+            h = pair_ref[pairing_row, g]
+            partner = stack_ref[h]
+            mean_partner = mean_ref[h]
+            spread_partner = spread_ref[h]
+            cross_term = box_rows(own * partner) - mean_own * mean_partner
+            factor = 2.0 * cross_term / jnp.maximum(spread_own * spread_partner, floor_product)
+            ratio_term = cross_term / guarded_spread
+            pair_term = factor * (partner[1:-1] - mean_partner - ratio_term * center_own)
+            drive_sum = pair_term if drive_sum is None else drive_sum + pair_term
+        out_ref[g] = drive_sum
+        return carry
+
+    lax.fori_loop(0, groups, pairs, 0)
+
+
+def slice_drive(stack, pairings):
+    groups, rows, y_rows, z_rows = stack.shape
+    shape = (groups, rows - 2, y_rows, z_rows)
+    return pl.pallas_call(
+        drive_kernel,
+        out_shape=jax.ShapeDtypeStruct(shape, jnp.float32),
+        in_specs=[
+            pl.BlockSpec(memory_space=pltpu.SMEM),
+            pl.BlockSpec(memory_space=pltpu.VMEM),
+        ],
+        out_specs=pl.BlockSpec(memory_space=pltpu.VMEM),
+        scratch_shapes=[pltpu.VMEM(shape, jnp.float32), pltpu.VMEM(shape, jnp.float32)],
+    )(pairings, stack)
 
 
 def advect_rows(near_own, velocity):
@@ -117,15 +148,14 @@
     groups = lax.axis_size("img")
     own = images[0]
     x_rows, y_rows, _ = own.shape
-    rows = y_rows // groups
+    rows = x_rows // groups
     own_ext = halo_rows(own, RADIUS + 1)
     near = own_ext[RADIUS:-RADIUS]
-    padded = jnp.pad(near, ((0, 0), (Y_MARGIN, Y_MARGIN), (0, 0)))
-    width = rows + 2 * Y_MARGIN
-    pieces = jnp.stack([padded[:, j * rows:j * rows + width] for j in range(groups)])
+    pieces = jnp.stack([near[j * rows:j * rows + rows + 2] for j in range(groups)])
     stack = lax.all_to_all(pieces, "img", split_axis=0, concat_axis=0, tiled=True)
-    drive_part = slice_drive(stack, pairings, rows)
-    drive_sum = lax.all_to_all(drive_part, "img", split_axis=0, concat_axis=2, tiled=True)[0]
+    drive_part = slice_drive(stack, pairings)
+    returned = lax.all_to_all(drive_part, "img", split_axis=0, concat_axis=0, tiled=True)
+    drive_sum = returned.reshape(own.shape)
     drive_ext = halo_rows(drive_sum, RADIUS)
     center = own_ext[1:-1]
     gradient = jnp.stack(

time: 181 us -> 132 us (0.73)
  the two profiles are of different devices: /device:TPU:6 before, /device:TPU:65 now
where the time goes in v2:
time: 132 us; the launch traced here: 131 us
  waiting for transfers between devices  35.7 us (27%)
  other arithmetic  31.1 us (24%)
  starting transfers between devices  27.2 us (21%)
  blocking collectives  24.7 us (19%)
  Pallas kernels  6.52 us (5%)
  local copies, waits for them, and re-layouts  5.08 us (4%)
    all_to_all x1, blocking collectives, shards(): lax.all_to_all(pieces, 'img', split_axis=0, concat_axis=0, tiled=True)  24.7 us
    ppermute x2, starting transfers between devices, halo_rows(): before = lax.ppermute(value[-width:], 'space', up)  19.1 us
    ppermute x2, waiting for transfers between devices, halo_rows(): after = lax.ppermute(value[:width], 'space', down)  17.9 us
    all_to_all x1, waiting for transfers between devices, shards(): lax.all_to_all(drive_part, 'img', split_axis=0, concat_axis=0, tiled=True)  12.3 us
    broadcast_in_dim x2, other arithmetic, shards(): return (advected[None], velocity[None])  11.2 us
    mul x1, other arithmetic, shards(): velocity = step_scale * smoothed  7.51 us
    pallas_call x1, Pallas kernels, slice_drive(): pl.pallas_call(drive_kernel, out_shape=jax.ShapeDtypeStruct(shape, jnp.fl...  6.52 us
    ppermute x2, waiting for transfers between devices, halo_rows(): before = lax.ppermute(value[-width:], 'space', up)  5.49 us
  transfers between devices with their start and end apart: 5, of which 4 were waited for; matrix products, arithmetic and copies ran while one was open for 1% of the time, Pallas kernels for 0%

profile of v2, /device:TPU:65, one launch (start us, length us, event | category | flops | bytes accessed | tf_op | source)
XLA Modules:
  0.0 131.1 jit_solution(14169966868874077591)
XLA Ops:
  0.6 1.1 slice_bitcast_fusion.1
  1.7 6.7 %collective-permute-start = (f32[5,96,128]{2,1,0:T(8,128)S(1)}, f32[5,96,128]{2,1,0:T(8,128)S(1)}, u32[]{:S(2)}, u32[]{:S(2)}) collective-permute-start(f32[5,96,128]{2,1,0:T(8,128)S(1)} %slice_bitcast_fusion.1), channel_id=1, source_target_pairs={{0,1},{1,2},{2,3},{3,4},{4,5},{5,6},{6,7},{7,8},{8,9},{9,10},{10,1... | collective-permute-start | bytes 737288 | tf_op jit(solution)/shard_map/ppermute | solution.py:32
  8.4 5.5 %collective-permute-done = f32[5,96,128]{2,1,0:T(8,128)S(1)} collective-permute-done((f32[5,96,128]{2,1,0:T(8,128)S(1)}, f32[5,96,128]{2,1,0:T(8,128)S(1)}, u32[]{:S(2)}, u32[]{:S(2)}) %collective-permute-start) | collective-permute-done | bytes 245792 | tf_op jit(solution)/shard_map/ppermute | solution.py:32
  13.9 0.9 fusion.58
  14.8 1.0 slice_dynamic-update-slice_fusion.5
  15.8 1.0 slice_dynamic-update-slice_fusion.4
  16.7 1.0 slice_dynamic-update-slice_fusion.3
  17.8 1.9 %collective-permute-start.1 = (f32[5,96,128]{2,1,0:T(8,128)S(1)}, f32[5,96,128]{2,1,0:T(8,128)S(1)}, u32[]{:S(2)}, u32[]{:S(2)}) collective-permute-start(f32[5,96,128]{2,1,0:T(8,128)S(1)} %get-tuple-element.9), channel_id=1, source_target_pairs={{1,0},{2,1},{3,2},{4,3},{5,4},{6,5},{7,6},{8,7},{9,8},{10,9},{11,1... | collective-permute-start | bytes 737288 | tf_op jit(solution)/shard_map/ppermute | solution.py:33
  19.8 10.1 %collective-permute-done.1 = f32[5,96,128]{2,1,0:T(8,128)S(1)} collective-permute-done((f32[5,96,128]{2,1,0:T(8,128)S(1)}, f32[5,96,128]{2,1,0:T(8,128)S(1)}, u32[]{:S(2)}, u32[]{:S(2)}) %collective-permute-start.1) | collective-permute-done | bytes 245792 | tf_op jit(solution)/shard_map/ppermute | solution.py:33
  29.9 24.7 %all_to_all.10.stack_ref = f32[8,5,96,128]{3,2,1,0:T(8,128)} all-to-all(f32[8,5,96,128]{3,2,1,0:T(8,128)S(1)} %fusion.57), channel_id=1, replica_groups=mesh['img'=8,'space'=32] {'img'}, dimensions={0} | all-to-all | bytes 3932160 | tf_op jit(solution)/shard_map/all_to_all | solution.py:155
  54.7 6.5 %shard_map.41 = f32[8,3,96,128]{3,2,1,0:T(8,128)} custom-call(s32[3,8]{1,0:T(4,128)} %pair_ref.1, f32[8,5,96,128]{3,2,1,0:T(8,128)} %all_to_all.10.stack_ref), custom_call_target="tpu_custom_call" | custom-call | tf_op jit(solution)/shard_map/pallas_call | solution.py:117
  61.2 4.3 %all-to-all-start.1 = ((f32[8,3,96,128]{3,2,1,0:T(8,128)}), f32[8,3,96,128]{3,2,1,0:T(8,128)}, u32[]{:S(2)}, u32[]{:S(2)}) async-start(f32[8,3,96,128]{3,2,1,0:T(8,128)} %shard_map.41), calls=%async_computation.1 | async-start | bytes 2359296 | tf_op jit(solution)/shard_map/all_to_all | solution.py:157
  65.5 12.3 %all-to-all-done.1 = f32[8,3,96,128]{3,2,1,0:T(8,128)} async-done(((f32[8,3,96,128]{3,2,1,0:T(8,128)}), f32[8,3,96,128]{3,2,1,0:T(8,128)}, u32[]{:S(2)}, u32[]{:S(2)}) %all-to-all-start.1) | async-done | bytes 1179680 | tf_op jit(solution)/shard_map/all_to_all | solution.py:157
  77.8 1.0 fusion.59
  78.9 12.4 %collective-permute-start.2 = (f32[4,96,128]{2,1,0:T(8,128)S(1)}, f32[4,96,128]{2,1,0:T(8,128)S(1)}, u32[]{:S(2)}, u32[]{:S(2)}) collective-permute-start(f32[4,96,128]{2,1,0:T(8,128)S(1)} %get-tuple-element.6), channel_id=1, source_target_pairs={{0,1},{1,2},{2,3},{3,4},{4,5},{5,6},{6,7},{7,8},{8,9},{9,10},{10,1... | collective-permute-start | bytes 589832 | tf_op jit(solution)/shard_map/ppermute | solution.py:32
  91.3 1.9 %collective-permute-start.3 = (f32[4,96,128]{2,1,0:T(8,128)S(1)}, f32[4,96,128]{2,1,0:T(8,128)S(1)}, u32[]{:S(2)}, u32[]{:S(2)}) collective-permute-start(f32[4,96,128]{2,1,0:T(8,128)S(1)} %get-tuple-element.7), channel_id=1, source_target_pairs={{1,0},{2,1},{3,2},{4,3},{5,4},{6,5},{7,6},{8,7},{9,8},{10,9},{11,1... | collective-permute-start | bytes 589832 | tf_op jit(solution)/shard_map/ppermute | solution.py:33
  93.6 1.1 fusion.32
  94.7 7.8 %collective-permute-done.3 = f32[4,96,128]{2,1,0:T(8,128)S(1)} collective-permute-done((f32[4,96,128]{2,1,0:T(8,128)S(1)}, f32[4,96,128]{2,1,0:T(8,128)S(1)}, u32[]{:S(2)}, u32[]{:S(2)}) %collective-permute-start.3) | collective-permute-done | bytes 196640 | tf_op jit(solution)/shard_map/ppermute | solution.py:33
  102.5 1.4 %pad_maximum_fusion.1 = f32[32,96,128]{2,1,0:T(8,128)S(1)} fusion(f32[4,96,128]{2,1,0:T(8,128)S(1)} %collective-permute-done.3, f32[24,96,128]{2,1,0:T(8,128)} %bitcast.5, f32[4,96,128]{2,1,0:T(8,128)S(1)} %collective-permute-done.2), kind=kLoop, calls=%fused_computation.68 | loop fusion | flops 786432 | bytes 3145728 | tf_op jit(solution)/shard_map/concatenate | solution.py:34
  104.5 4.0 %fusion.17 = f32[3,24,96,128]{3,2,1,0:T(8,128)S(1)} fusion(f32[3,32,96,128]{3,2,1,0:T(8,128)S(1)} %maximum_multiply_fusion), kind=kLoop, calls=%fused_computation.29 | loop fusion | flops 15040512 | bytes 35389440 | tf_op jit(solution)/shard_map/add | solution.py:66
  108.6 3.8 %multiply_add_fusion = f32[3,24,96,128]{3,2,1,0:T(8,128)S(1)} fusion(f32[3,24,96,128]{3,2,1,0:T(8,128)S(1)} %fusion.17), kind=kLoop, calls=%fused_computation.45 | loop fusion | flops 15040512 | bytes 7077888 | tf_op jit(solution)/shard_map/add | solution.py:58
  112.4 8.7 %fusion.60 = f32[1,3,24,96,128]{4,3,2,1,0:T(8,128)} fusion(f32[3,24,96,128]{3,2,1,0:T(8,128)S(1)} %multiply_add_fusion), kind=kLoop, calls=%fused_computation.105 | loop fusion | flops 15925248 | bytes 7077888 | tf_op jit(solution)/shard_map/broadcast_in_dim | solution.py:170
  121.1 7.5 %fusion.9 = f32[3,24,96,128]{3,2,1,0:T(8,128)S(1)} fusion(f32[3,24,96,128]{3,2,1,0:T(8,128)S(1)} %multiply_add_fusion), kind=kLoop, calls=%fused_computation.20 | loop fusion | flops 15925248 | bytes 7077888 | tf_op jit(solution)/shard_map/mul | solution.py:168
  128.6 2.6 %fusion.44 = f32[1,24,96,128]{3,2,1,0:T(8,128)} fusion(f32[24,96,128]{2,1,0:T(8,128)S(1)} %bitcast.39, f32[5,96,128]{2,1,0:T(8,128)S(1)} %collective-permute-done.1, f32[5,96,128]{2,1,0:T(8,128)S(1)} %collective-permute-done, f32[3,24,96,128]{3,2,1,0:T(8,128)S(1)} %fusion.9), kind=kLoop, calls=%fused_computation.77 | loop fusion | flops 7667712 | bytes 6389760 | tf_op jit(solution)/shard_map/broadcast_in_dim | solution.py:170
  (10 shorter events, 1.2 us)
Async XLA Ops:
  0.6 17.1 %copy-start = (f32[1,24,96,128]{3,2,1,0:T(8,128)S(1)}, f32[1,24,96,128]{3,2,1,0:T(8,128)}, u32[]{:S(2)}) copy-start(f32[1,24,96,128]{3,2,1,0:T(8,128)} %param.2) | copy-start | bytes 3538948
  1.7 12.2 %collective-permute-start = (f32[5,96,128]{2,1,0:T(8,128)S(1)}, f32[5,96,128]{2,1,0:T(8,128)S(1)}, u32[]{:S(2)}, u32[]{:S(2)}) collective-permute-start(f32[5,96,128]{2,1,0:T(8,128)S(1)} %slice_bitcast_fusion.1), channel_id=1, source_target_pairs={{0,1},{1,2},{2,3},{3,4},{4,5},{5,6},{6,7},{7,8},{8,9},{9,10},{10,1... | collective-permute-start | bytes 737288 | tf_op jit(solution)/shard_map/ppermute | solution.py:32
  17.8 12.1 %collective-permute-start.1 = (f32[5,96,128]{2,1,0:T(8,128)S(1)}, f32[5,96,128]{2,1,0:T(8,128)S(1)}, u32[]{:S(2)}, u32[]{:S(2)}) collective-permute-start(f32[5,96,128]{2,1,0:T(8,128)S(1)} %get-tuple-element.9), channel_id=1, source_target_pairs={{1,0},{2,1},{3,2},{4,3},{5,4},{6,5},{7,6},{8,7},{9,8},{10,9},{11,1... | collective-permute-start | bytes 737288 | tf_op jit(solution)/shard_map/ppermute | solution.py:33
  61.2 16.6 %all-to-all-start.1 = ((f32[8,3,96,128]{3,2,1,0:T(8,128)}), f32[8,3,96,128]{3,2,1,0:T(8,128)}, u32[]{:S(2)}, u32[]{:S(2)}) async-start(f32[8,3,96,128]{3,2,1,0:T(8,128)} %shard_map.41), calls=%async_computation.1 | async-start | bytes 2359296 | tf_op jit(solution)/shard_map/all_to_all | solution.py:157
  78.9 15.8 %collective-permute-start.2 = (f32[4,96,128]{2,1,0:T(8,128)S(1)}, f32[4,96,128]{2,1,0:T(8,128)S(1)}, u32[]{:S(2)}, u32[]{:S(2)}) collective-permute-start(f32[4,96,128]{2,1,0:T(8,128)S(1)} %get-tuple-element.6), channel_id=1, source_target_pairs={{0,1},{1,2},{2,3},{3,4},{4,5},{5,6},{6,7},{7,8},{8,9},{9,10},{10,1... | collective-permute-start | bytes 589832 | tf_op jit(solution)/shard_map/ppermute | solution.py:32
  91.3 11.2 %collective-permute-start.3 = (f32[4,96,128]{2,1,0:T(8,128)S(1)}, f32[4,96,128]{2,1,0:T(8,128)S(1)}, u32[]{:S(2)}, u32[]{:S(2)}) collective-permute-start(f32[4,96,128]{2,1,0:T(8,128)S(1)} %get-tuple-element.7), channel_id=1, source_target_pairs={{1,0},{2,1},{3,2},{4,3},{5,4},{6,5},{7,6},{8,7},{9,8},{10,9},{11,1... | collective-permute-start | bytes 589832 | tf_op jit(solution)/shard_map/ppermute | solution.py:33

commit v3 on v2

--- a/solution.py
+++ b/solution.py
@@ -1,6 +1,7 @@
 import math
 
 import jax
+import numpy as np
 import jax.numpy as jnp
 from jax import lax
 from jax.experimental import pallas as pl
@@ -143,6 +144,85 @@
     return center - change
 
 
+def shifted(value, offset, axis):
+    length = value.shape[axis]
+    rolled = pltpu.roll(value, (-offset) % length, axis)
+    index = lax.broadcasted_iota(jnp.int32, value.shape, axis) + offset
+    return jnp.where((index >= 0) & (index < length), rolled, 0.0)
+
+
+def post_kernel(drive_ref, own_ref, wy_ref, wz_ref, vel_ref, adv_ref, force_ref):
+    extended = drive_ref.shape[0]
+    x_rows = vel_ref.shape[1]
+    taps = gauss_taps(RADIUS)
+    highest = lax.Precision.HIGHEST
+
+    def force_row(r, carry):
+        value = own_ref[r + 1]
+        drive = drive_ref[r]
+        force_ref[0, r] = drive * ((own_ref[r + 2] - own_ref[r]) * 0.5)
+        force_ref[1, r] = drive * ((shifted(value, 1, 0) - shifted(value, -1, 0)) * 0.5)
+        force_ref[2, r] = drive * ((shifted(value, 1, 1) - shifted(value, -1, 1)) * 0.5)
+        return carry
+
+    lax.fori_loop(0, extended, force_row, 0)
+    wy = wy_ref[...]
+    wz = wz_ref[...]
+
+    def out_row(x, carry):
+        value = own_ref[x + RADIUS + 1]
+        change = None
+        for c in range(3):
+            acc = taps[0] * force_ref[c, x]
+            for t in range(1, len(taps)):
+                acc = acc + taps[t] * force_ref[c, x + t]
+            acc = jnp.dot(wy, acc, precision=highest, preferred_element_type=jnp.float32)
+            acc = jnp.dot(acc, wz, precision=highest, preferred_element_type=jnp.float32)
+            speed = step_scale * acc
+            vel_ref[c, x] = speed
+            if c == 0:
+                backward = value - own_ref[x + RADIUS]
+                forward = own_ref[x + RADIUS + 2] - value
+            else:
+                backward = value - shifted(value, -1, c - 1)
+                forward = shifted(value, 1, c - 1) - value
+            part = jnp.maximum(speed, 0.0) * backward + jnp.minimum(speed, 0.0) * forward
+            change = part if change is None else change + part
+        adv_ref[x] = value - change
+        return carry
+
+    lax.fori_loop(0, x_rows, out_row, 0)
+
+
+def band(length, taps):
+    radius = len(taps) // 2
+    matrix = np.zeros((length, length), np.float32)
+    for i in range(length):
+        for t in range(-radius, radius + 1):
+            if 0 <= i + t < length:
+                matrix[i, i + t] = taps[t + radius]
+    return matrix
+
+
+def post_stage(drive_ext, own_ext):
+    extended, y_rows, z_rows = drive_ext.shape
+    x_rows = extended - 2 * RADIUS
+    taps = gauss_taps(RADIUS)
+    wy = jnp.asarray(band(y_rows, taps))
+    wz = jnp.asarray(band(z_rows, taps).T)
+    vmem = pl.BlockSpec(memory_space=pltpu.VMEM)
+    return pl.pallas_call(
+        post_kernel,
+        out_shape=(
+            jax.ShapeDtypeStruct((3, x_rows, y_rows, z_rows), jnp.float32),
+            jax.ShapeDtypeStruct((x_rows, y_rows, z_rows), jnp.float32),
+        ),
+        in_specs=[vmem] * 4,
+        out_specs=(vmem, vmem),
+        scratch_shapes=[pltpu.VMEM((3, extended, y_rows, z_rows), jnp.float32)],
+    )(drive_ext, own_ext, wy, wz)
+
+
 def shards(images, pairings):
     weights = gauss_taps(RADIUS)
     groups = lax.axis_size("img")
@@ -157,16 +237,7 @@
     returned = lax.all_to_all(drive_part, "img", split_axis=0, concat_axis=0, tiled=True)
     drive_sum = returned.reshape(own.shape)
     drive_ext = halo_rows(drive_sum, RADIUS)
-    center = own_ext[1:-1]
-    gradient = jnp.stack(
-        [(own_ext[2:] - own_ext[:-2]) * 0.5, central(center, 1), central(center, 2)]
-    )
-    force = drive_ext[None] * gradient
-    smoothed = smooth_rows(force, weights)
-    smoothed = smooth_along(smoothed, 2, weights)
-    smoothed = smooth_along(smoothed, 3, weights)
-    velocity = step_scale * smoothed
-    advected = advect_rows(near, velocity)
+    velocity, advected = post_stage(drive_ext, own_ext)
     return (advected[None], velocity[None])
 
 

time: 132 us -> 126 us (0.955)
  the two profiles are of different devices: /device:TPU:65 before, /device:TPU:69 now
where the time goes in v3:
time: 126 us
  blocking collectives  41.5 us (33%)
  Pallas kernels  32.4 us (26%)
  waiting for transfers between devices  23.6 us (19%)
  starting transfers between devices  22.8 us (18%)
  other arithmetic  3.52 us (3%)
    pallas_call x1, Pallas kernels, post_stage(): pl.pallas_call(post_kernel, out_shape=(jax.ShapeDtypeStruct((3, x_rows, y...  25.8 us
    all_to_all x1, blocking collectives, shards(): lax.all_to_all(pieces, 'img', split_axis=0, concat_axis=0, tiled=True)  24.7 us
    ppermute x2, starting transfers between devices, halo_rows(): before = lax.ppermute(value[-width:], 'space', up)  19 us
    ppermute x2, waiting for transfers between devices, halo_rows(): after = lax.ppermute(value[:width], 'space', down)  18.1 us
    all_to_all x1, blocking collectives, shards(): lax.all_to_all(drive_part, 'img', split_axis=0, concat_axis=0, tiled=True)  16.8 us
    pallas_call x1, Pallas kernels, slice_drive(): pl.pallas_call(drive_kernel, out_shape=jax.ShapeDtypeStruct(shape, jnp.fl...  6.52 us
    ppermute x2, waiting for transfers between devices, halo_rows(): before = lax.ppermute(value[-width:], 'space', up)  5.49 us
    ppermute x2, starting transfers between devices, halo_rows(): after = lax.ppermute(value[:width], 'space', down)  3.84 us
  transfers between devices with their start and end apart: 4, of which 3 were waited for; matrix products, arithmetic and copies ran while one was open for 1% of the time, Pallas kernels for 0%

profile of v3, /device:TPU:69, one launch (start us, length us, event | category | flops | bytes accessed | tf_op | source)
XLA Modules:
  0.0 125.7 jit_solution(9454625295423650072)
XLA Ops:
  0.6 0.0 copy-start
  0.6 1.1 slice_bitcast_fusion.1
  1.7 6.7 %collective-permute-start = (f32[5,96,128]{2,1,0:T(8,128)S(1)}, f32[5,96,128]{2,1,0:T(8,128)S(1)}, u32[]{:S(2)}, u32[]{:S(2)}) collective-permute-start(f32[5,96,128]{2,1,0:T(8,128)S(1)} %slice_bitcast_fusion.1), channel_id=1, source_target_pairs={{0,1},{1,2},{2,3},{3,4},{4,5},{5,6},{6,7},{7,8},{8,9},{9,10},{10,1... | collective-permute-start | bytes 737288 | tf_op jit(solution)/shard_map/ppermute | solution.py:33
  8.4 5.5 %collective-permute-done = f32[5,96,128]{2,1,0:T(8,128)S(1)} collective-permute-done((f32[5,96,128]{2,1,0:T(8,128)S(1)}, f32[5,96,128]{2,1,0:T(8,128)S(1)}, u32[]{:S(2)}, u32[]{:S(2)}) %collective-permute-start) | collective-permute-done | bytes 245792 | tf_op jit(solution)/shard_map/ppermute | solution.py:33
  13.9 0.9 fusion.3
  14.8 0.0 copy-done
  15.0 1.9 %collective-permute-start.1 = (f32[5,96,128]{2,1,0:T(8,128)S(1)}, f32[5,96,128]{2,1,0:T(8,128)S(1)}, u32[]{:S(2)}, u32[]{:S(2)}) collective-permute-start(f32[5,96,128]{2,1,0:T(8,128)S(1)} %get-tuple-element.8), channel_id=1, source_target_pairs={{1,0},{2,1},{3,2},{4,3},{5,4},{6,5},{7,6},{8,7},{9,8},{10,9},{11,1... | collective-permute-start | bytes 737288 | tf_op jit(solution)/shard_map/ppermute | solution.py:34
  16.9 10.1 %collective-permute-done.1 = f32[5,96,128]{2,1,0:T(8,128)S(1)} collective-permute-done((f32[5,96,128]{2,1,0:T(8,128)S(1)}, f32[5,96,128]{2,1,0:T(8,128)S(1)}, u32[]{:S(2)}, u32[]{:S(2)}) %collective-permute-start.1) | collective-permute-done | bytes 245792 | tf_op jit(solution)/shard_map/ppermute | solution.py:34
  27.1 24.7 %all_to_all.10.stack_ref = f32[8,5,96,128]{3,2,1,0:T(8,128)} all-to-all(f32[8,5,96,128]{3,2,1,0:T(8,128)S(1)} %fusion.1), channel_id=1, replica_groups=mesh['img'=8,'space'=32] {'img'}, dimensions={0} | all-to-all | bytes 3932160 | tf_op jit(solution)/shard_map/all_to_all | solution.py:235
  51.8 6.5 %shard_map.59 = f32[8,3,96,128]{3,2,1,0:T(8,128)} custom-call(s32[3,8]{1,0:T(4,128)} %pair_ref.1, f32[8,5,96,128]{3,2,1,0:T(8,128)} %all_to_all.10.stack_ref), custom_call_target="tpu_custom_call" | custom-call | tf_op jit(solution)/shard_map/pallas_call | solution.py:118
  58.3 16.8 %all_to_all.11 = f32[8,3,96,128]{3,2,1,0:T(8,128)S(1)} all-to-all(f32[8,3,96,128]{3,2,1,0:T(8,128)} %shard_map.59), channel_id=1, replica_groups=mesh['img'=8,'space'=32] {'img'}, dimensions={0} | all-to-all | bytes 2359296 | tf_op jit(solution)/shard_map/all_to_all | solution.py:237
  75.1 12.3 %collective-permute-start.2 = (f32[4,96,128]{2,1,0:T(8,128)S(1)}, f32[4,96,128]{2,1,0:T(8,128)S(1)}, u32[]{:S(2)}, u32[]{:S(2)}) collective-permute-start(f32[4,96,128]{2,1,0:T(8,128)S(1)} %get-tuple-element.6), channel_id=1, source_target_pairs={{0,1},{1,2},{2,3},{3,4},{4,5},{5,6},{6,7},{7,8},{8,9},{9,10},{10,1... | collective-permute-start | bytes 589832 | tf_op jit(solution)/shard_map/ppermute | solution.py:33
  87.4 1.9 %collective-permute-start.3 = (f32[4,96,128]{2,1,0:T(8,128)S(1)}, f32[4,96,128]{2,1,0:T(8,128)S(1)}, u32[]{:S(2)}, u32[]{:S(2)}) collective-permute-start(f32[4,96,128]{2,1,0:T(8,128)S(1)} %get-tuple-element.7), channel_id=1, source_target_pairs={{1,0},{2,1},{3,2},{4,3},{5,4},{6,5},{7,6},{8,7},{9,8},{10,9},{11,1... | collective-permute-start | bytes 589832 | tf_op jit(solution)/shard_map/ppermute | solution.py:34
  89.4 1.3 %pad_maximum_fusion.own_ref = f32[34,96,128]{2,1,0:T(8,128)} fusion(f32[5,96,128]{2,1,0:T(8,128)S(1)} %collective-permute-done.1, f32[24,96,128]{2,1,0:T(8,128)S(1)} %bitcast.18, f32[5,96,128]{2,1,0:T(8,128)S(1)} %collective-permute-done), kind=kLoop, calls=%fused_computation | loop fusion | flops 835584 | bytes 3342336 | tf_op jit(solution)/shard_map/concatenate | solution.py:35
  90.7 0.0 collective-permute-done.2
  90.7 8.0 %collective-permute-done.3 = f32[4,96,128]{2,1,0:T(8,128)S(1)} collective-permute-done((f32[4,96,128]{2,1,0:T(8,128)S(1)}, f32[4,96,128]{2,1,0:T(8,128)S(1)}, u32[]{:S(2)}, u32[]{:S(2)}) %collective-permute-start.3) | collective-permute-done | bytes 196640 | tf_op jit(solution)/shard_map/ppermute | solution.py:34
  98.6 1.3 pad_maximum_fusion.1.drive_ref
  99.9 25.8 %shard_map.60 = (f32[3,24,96,128]{3,2,1,0:T(8,128)}, f32[24,96,128]{2,1,0:T(8,128)}) custom-call(f32[32,96,128]{2,1,0:T(8,128)} %pad_maximum_fusion.1.drive_ref, f32[34,96,128]{2,1,0:T(8,128)} %pad_maximum_fusion.own_ref, f32[96,96]{1,0:T(8,128)} %constant.4.clone.wy_ref, f32[128,128]{1,0:T(8,128)} %constant.5.clone.wz_ref), custom_call_target="tpu_custom_call" | custom-call | tf_op jit(solution)/shard_map/pallas_call | solution.py:214
  (8 shorter events, 0.2 us)
Async XLA Ops:
  0.6 14.2 %copy-start = (f32[1,24,96,128]{3,2,1,0:T(8,128)S(1)}, f32[1,24,96,128]{3,2,1,0:T(8,128)}, u32[]{:S(2)}) copy-start(f32[1,24,96,128]{3,2,1,0:T(8,128)} %param.4) | copy-start | bytes 3538948
  1.7 12.2 %collective-permute-start = (f32[5,96,128]{2,1,0:T(8,128)S(1)}, f32[5,96,128]{2,1,0:T(8,128)S(1)}, u32[]{:S(2)}, u32[]{:S(2)}) collective-permute-start(f32[5,96,128]{2,1,0:T(8,128)S(1)} %slice_bitcast_fusion.1), channel_id=1, source_target_pairs={{0,1},{1,2},{2,3},{3,4},{4,5},{5,6},{6,7},{7,8},{8,9},{9,10},{10,1... | collective-permute-start | bytes 737288 | tf_op jit(solution)/shard_map/ppermute | solution.py:33
  15.0 12.1 %collective-permute-start.1 = (f32[5,96,128]{2,1,0:T(8,128)S(1)}, f32[5,96,128]{2,1,0:T(8,128)S(1)}, u32[]{:S(2)}, u32[]{:S(2)}) collective-permute-start(f32[5,96,128]{2,1,0:T(8,128)S(1)} %get-tuple-element.8), channel_id=1, source_target_pairs={{1,0},{2,1},{3,2},{4,3},{5,4},{6,5},{7,6},{8,7},{9,8},{10,9},{11,1... | collective-permute-start | bytes 737288 | tf_op jit(solution)/shard_map/ppermute | solution.py:34
  75.1 15.5 %collective-permute-start.2 = (f32[4,96,128]{2,1,0:T(8,128)S(1)}, f32[4,96,128]{2,1,0:T(8,128)S(1)}, u32[]{:S(2)}, u32[]{:S(2)}) collective-permute-start(f32[4,96,128]{2,1,0:T(8,128)S(1)} %get-tuple-element.6), channel_id=1, source_target_pairs={{0,1},{1,2},{2,3},{3,4},{4,5},{5,6},{6,7},{7,8},{8,9},{9,10},{10,1... | collective-permute-start | bytes 589832 | tf_op jit(solution)/shard_map/ppermute | solution.py:33
  87.4 11.2 %collective-permute-start.3 = (f32[4,96,128]{2,1,0:T(8,128)S(1)}, f32[4,96,128]{2,1,0:T(8,128)S(1)}, u32[]{:S(2)}, u32[]{:S(2)}) collective-permute-start(f32[4,96,128]{2,1,0:T(8,128)S(1)} %get-tuple-element.7), channel_id=1, source_target_pairs={{1,0},{2,1},{3,2},{4,3},{5,4},{6,5},{7,6},{8,7},{9,8},{10,9},{11,1... | collective-permute-start | bytes 589832 | tf_op jit(solution)/shard_map/ppermute | solution.py:34

commit v4 on v3

--- a/solution.py
+++ b/solution.py
@@ -151,33 +151,59 @@
     return jnp.where((index >= 0) & (index < length), rolled, 0.0)
 
 
-def post_kernel(drive_ref, own_ref, wy_ref, wz_ref, vel_ref, adv_ref, force_ref):
-    extended = drive_ref.shape[0]
+def post_kernel(drive_ref, own_ref, wz_ref, vel_ref, adv_ref, force_ref, pass_ref):
+    extended, y_rows, _ = drive_ref.shape
     x_rows = vel_ref.shape[1]
     taps = gauss_taps(RADIUS)
-    highest = lax.Precision.HIGHEST
+
+    def plane(c, r, count):
+        return pl.ds(pl.multiple_of((c * count + r) * y_rows, 8), y_rows)
 
     def force_row(r, carry):
         value = own_ref[r + 1]
         drive = drive_ref[r]
-        force_ref[0, r] = drive * ((own_ref[r + 2] - own_ref[r]) * 0.5)
-        force_ref[1, r] = drive * ((shifted(value, 1, 0) - shifted(value, -1, 0)) * 0.5)
-        force_ref[2, r] = drive * ((shifted(value, 1, 1) - shifted(value, -1, 1)) * 0.5)
+        force_ref[plane(0, r, extended)] = drive * ((own_ref[r + 2] - own_ref[r]) * 0.5)
+        force_ref[plane(1, r, extended)] = drive * (
+            (shifted(value, 1, 0) - shifted(value, -1, 0)) * 0.5
+        )
+        force_ref[plane(2, r, extended)] = drive * (
+            (shifted(value, 1, 1) - shifted(value, -1, 1)) * 0.5
+        )
         return carry
 
     lax.fori_loop(0, extended, force_row, 0)
-    wy = wy_ref[...]
+
+    def x_pass(x, carry):
+        for c in range(3):
+            acc = taps[0] * force_ref[plane(c, x, extended)]
+            for t in range(1, len(taps)):
+                acc = acc + taps[t] * force_ref[plane(c, x + t, extended)]
+            pass_ref[plane(c, x, x_rows)] = acc
+        return carry
+
+    lax.fori_loop(0, x_rows, x_pass, 0)
     wz = wz_ref[...]
+    chunk = 8 * y_rows
+    chunks = pass_ref.shape[0] // chunk
+
+    def z_pass(i, carry):
+        rows = pl.ds(pl.multiple_of(i * chunk, 8), chunk)
+        pass_ref[rows] = jnp.dot(
+            pass_ref[rows], wz, precision=lax.Precision.HIGHEST,
+            preferred_element_type=jnp.float32,
+        )
+        return carry
+
+    lax.fori_loop(0, chunks, z_pass, 0)
 
     def out_row(x, carry):
         value = own_ref[x + RADIUS + 1]
         change = None
         for c in range(3):
-            acc = taps[0] * force_ref[c, x]
+            smoothed_z = pass_ref[plane(c, x, x_rows)]
+            acc = taps[0] * shifted(smoothed_z, -RADIUS, 0)
             for t in range(1, len(taps)):
-                acc = acc + taps[t] * force_ref[c, x + t]
-            acc = jnp.dot(wy, acc, precision=highest, preferred_element_type=jnp.float32)
-            acc = jnp.dot(acc, wz, precision=highest, preferred_element_type=jnp.float32)
+                acc = acc + taps[t] * shifted(smoothed_z, t - RADIUS, 0)
             speed = step_scale * acc
             vel_ref[c, x] = speed
             if c == 0:
@@ -208,7 +234,6 @@
     extended, y_rows, z_rows = drive_ext.shape
     x_rows = extended - 2 * RADIUS
     taps = gauss_taps(RADIUS)
-    wy = jnp.asarray(band(y_rows, taps))
     wz = jnp.asarray(band(z_rows, taps).T)
     vmem = pl.BlockSpec(memory_space=pltpu.VMEM)
     return pl.pallas_call(
@@ -217,10 +242,13 @@
             jax.ShapeDtypeStruct((3, x_rows, y_rows, z_rows), jnp.float32),
             jax.ShapeDtypeStruct((x_rows, y_rows, z_rows), jnp.float32),
         ),
-        in_specs=[vmem] * 4,
+        in_specs=[vmem] * 3,
         out_specs=(vmem, vmem),
-        scratch_shapes=[pltpu.VMEM((3, extended, y_rows, z_rows), jnp.float32)],
-    )(drive_ext, own_ext, wy, wz)
+        scratch_shapes=[
+            pltpu.VMEM((3 * extended * y_rows, z_rows), jnp.float32),
+            pltpu.VMEM((3 * x_rows * y_rows, z_rows), jnp.float32),
+        ],
+    )(drive_ext, own_ext, wz)
 
 
 def shards(images, pairings):

time: 126 us -> 119 us (0.944)
  Pallas kernels: 32.4 us -> 25.7 us
    pallas_call x1, Pallas kernels: 25.8 us -> 19.2 us  [post_stage(): pl.pallas_call(post_kernel, out_shape=(jax.ShapeDtypeStruct((3, x_rows, y...]
where the time goes in v4:
time: 119 us
  blocking collectives  41.5 us (35%)
  Pallas kernels  25.7 us (22%)
  waiting for transfers between devices  23.6 us (20%)
  starting transfers between devices  22.8 us (19%)
  other arithmetic  3.52 us (3%)
  local copies, waits for them, and re-layouts  1.22 us (1%)
    all_to_all x1, blocking collectives, shards(): lax.all_to_all(pieces, 'img', split_axis=0, concat_axis=0, tiled=True)  24.7 us
    pallas_call x1, Pallas kernels, post_stage(): pl.pallas_call(post_kernel, out_shape=(jax.ShapeDtypeStruct((3, x_rows, y...  19.2 us
    ppermute x2, starting transfers between devices, halo_rows(): before = lax.ppermute(value[-width:], 'space', up)  19 us
    ppermute x2, waiting for transfers between devices, halo_rows(): after = lax.ppermute(value[:width], 'space', down)  18.1 us
    all_to_all x1, blocking collectives, shards(): lax.all_to_all(drive_part, 'img', split_axis=0, concat_axis=0, tiled=True)  16.8 us
    pallas_call x1, Pallas kernels, slice_drive(): pl.pallas_call(drive_kernel, out_shape=jax.ShapeDtypeStruct(shape, jnp.fl...  6.52 us
    ppermute x2, waiting for transfers between devices, halo_rows(): before = lax.ppermute(value[-width:], 'space', up)  5.49 us
    ppermute x2, starting transfers between devices, halo_rows(): after = lax.ppermute(value[:width], 'space', down)  3.84 us
  transfers between devices with their start and end apart: 4, of which 3 were waited for; matrix products, arithmetic and copies ran while one was open for 1% of the time, Pallas kernels for 0%

profile of v4, /device:TPU:69, one launch (start us, length us, event | category | flops | bytes accessed | tf_op | source)
XLA Modules:
  0.0 119.1 jit_solution(7451082864968103291)
XLA Ops:
  0.6 0.0 copy-start
  0.6 1.1 slice_bitcast_fusion.1
  1.7 6.7 %collective-permute-start = (f32[5,96,128]{2,1,0:T(8,128)S(1)}, f32[5,96,128]{2,1,0:T(8,128)S(1)}, u32[]{:S(2)}, u32[]{:S(2)}) collective-permute-start(f32[5,96,128]{2,1,0:T(8,128)S(1)} %slice_bitcast_fusion.1), channel_id=1, source_target_pairs={{0,1},{1,2},{2,3},{3,4},{4,5},{5,6},{6,7},{7,8},{8,9},{9,10},{10,1... | collective-permute-start | bytes 737288 | tf_op jit(solution)/shard_map/ppermute | solution.py:33
  8.4 5.5 %collective-permute-done = f32[5,96,128]{2,1,0:T(8,128)S(1)} collective-permute-done((f32[5,96,128]{2,1,0:T(8,128)S(1)}, f32[5,96,128]{2,1,0:T(8,128)S(1)}, u32[]{:S(2)}, u32[]{:S(2)}) %collective-permute-start) | collective-permute-done | bytes 245792 | tf_op jit(solution)/shard_map/ppermute | solution.py:33
  13.9 0.9 fusion.3
  14.8 0.0 copy-done
  15.0 1.9 %collective-permute-start.1 = (f32[5,96,128]{2,1,0:T(8,128)S(1)}, f32[5,96,128]{2,1,0:T(8,128)S(1)}, u32[]{:S(2)}, u32[]{:S(2)}) collective-permute-start(f32[5,96,128]{2,1,0:T(8,128)S(1)} %get-tuple-element.8), channel_id=1, source_target_pairs={{1,0},{2,1},{3,2},{4,3},{5,4},{6,5},{7,6},{8,7},{9,8},{10,9},{11,1... | collective-permute-start | bytes 737288 | tf_op jit(solution)/shard_map/ppermute | solution.py:34
  16.9 10.1 %collective-permute-done.1 = f32[5,96,128]{2,1,0:T(8,128)S(1)} collective-permute-done((f32[5,96,128]{2,1,0:T(8,128)S(1)}, f32[5,96,128]{2,1,0:T(8,128)S(1)}, u32[]{:S(2)}, u32[]{:S(2)}) %collective-permute-start.1) | collective-permute-done | bytes 245792 | tf_op jit(solution)/shard_map/ppermute | solution.py:34
  27.1 24.7 %all_to_all.10.stack_ref = f32[8,5,96,128]{3,2,1,0:T(8,128)} all-to-all(f32[8,5,96,128]{3,2,1,0:T(8,128)S(1)} %fusion.1), channel_id=1, replica_groups=mesh['img'=8,'space'=32] {'img'}, dimensions={0} | all-to-all | bytes 3932160 | tf_op jit(solution)/shard_map/all_to_all | solution.py:263
  51.8 6.5 %shard_map.50 = f32[8,3,96,128]{3,2,1,0:T(8,128)} custom-call(s32[3,8]{1,0:T(4,128)} %pair_ref.1, f32[8,5,96,128]{3,2,1,0:T(8,128)} %all_to_all.10.stack_ref), custom_call_target="tpu_custom_call" | custom-call | tf_op jit(solution)/shard_map/pallas_call | solution.py:118
  58.3 16.8 %all_to_all.11 = f32[8,3,96,128]{3,2,1,0:T(8,128)S(1)} all-to-all(f32[8,3,96,128]{3,2,1,0:T(8,128)} %shard_map.50), channel_id=1, replica_groups=mesh['img'=8,'space'=32] {'img'}, dimensions={0} | all-to-all | bytes 2359296 | tf_op jit(solution)/shard_map/all_to_all | solution.py:265
  75.1 12.3 %collective-permute-start.2 = (f32[4,96,128]{2,1,0:T(8,128)S(1)}, f32[4,96,128]{2,1,0:T(8,128)S(1)}, u32[]{:S(2)}, u32[]{:S(2)}) collective-permute-start(f32[4,96,128]{2,1,0:T(8,128)S(1)} %get-tuple-element.6), channel_id=1, source_target_pairs={{0,1},{1,2},{2,3},{3,4},{4,5},{5,6},{6,7},{7,8},{8,9},{9,10},{10,1... | collective-permute-start | bytes 589832 | tf_op jit(solution)/shard_map/ppermute | solution.py:33
  87.4 1.9 %collective-permute-start.3 = (f32[4,96,128]{2,1,0:T(8,128)S(1)}, f32[4,96,128]{2,1,0:T(8,128)S(1)}, u32[]{:S(2)}, u32[]{:S(2)}) collective-permute-start(f32[4,96,128]{2,1,0:T(8,128)S(1)} %get-tuple-element.7), channel_id=1, source_target_pairs={{1,0},{2,1},{3,2},{4,3},{5,4},{6,5},{7,6},{8,7},{9,8},{10,9},{11,1... | collective-permute-start | bytes 589832 | tf_op jit(solution)/shard_map/ppermute | solution.py:34
  89.4 1.3 %pad_maximum_fusion.own_ref = f32[34,96,128]{2,1,0:T(8,128)} fusion(f32[5,96,128]{2,1,0:T(8,128)S(1)} %collective-permute-done.1, f32[24,96,128]{2,1,0:T(8,128)S(1)} %bitcast.18, f32[5,96,128]{2,1,0:T(8,128)S(1)} %collective-permute-done), kind=kLoop, calls=%fused_computation | loop fusion | flops 835584 | bytes 3342336 | tf_op jit(solution)/shard_map/concatenate | solution.py:35
  90.7 0.0 collective-permute-done.2
  90.7 8.0 %collective-permute-done.3 = f32[4,96,128]{2,1,0:T(8,128)S(1)} collective-permute-done((f32[4,96,128]{2,1,0:T(8,128)S(1)}, f32[4,96,128]{2,1,0:T(8,128)S(1)}, u32[]{:S(2)}, u32[]{:S(2)}) %collective-permute-start.3) | collective-permute-done | bytes 196640 | tf_op jit(solution)/shard_map/ppermute | solution.py:34
  98.6 1.3 %pad_maximum_fusion.1.drive_ref = f32[32,96,128]{2,1,0:T(8,128)} fusion(f32[4,96,128]{2,1,0:T(8,128)S(1)} %collective-permute-done.3, f32[24,96,128]{2,1,0:T(8,128)S(1)} %bitcast.20, f32[4,96,128]{2,1,0:T(8,128)S(1)} %collective-permute-done.2), kind=kLoop, calls=%fused_computation.1 | loop fusion | flops 786432 | bytes 3145728 | tf_op jit(solution)/shard_map/concatenate | solution.py:35
  99.9 19.2 %shard_map.51 = (f32[3,24,96,128]{3,2,1,0:T(8,128)}, f32[24,96,128]{2,1,0:T(8,128)}) custom-call(f32[32,96,128]{2,1,0:T(8,128)} %pad_maximum_fusion.1.drive_ref, f32[34,96,128]{2,1,0:T(8,128)} %pad_maximum_fusion.own_ref, f32[128,128]{1,0:T(8,128)} %constant.2.clone.wz_ref), custom_call_target="tpu_custom_call" | custom-call | tf_op jit(solution)/shard_map/pallas_call | solution.py:239
  (8 shorter events, 0.2 us)
Async XLA Ops:
  0.6 14.2 %copy-start = (f32[1,24,96,128]{3,2,1,0:T(8,128)S(1)}, f32[1,24,96,128]{3,2,1,0:T(8,128)}, u32[]{:S(2)}) copy-start(f32[1,24,96,128]{3,2,1,0:T(8,128)} %param.3) | copy-start | bytes 3538948
  1.7 12.2 %collective-permute-start = (f32[5,96,128]{2,1,0:T(8,128)S(1)}, f32[5,96,128]{2,1,0:T(8,128)S(1)}, u32[]{:S(2)}, u32[]{:S(2)}) collective-permute-start(f32[5,96,128]{2,1,0:T(8,128)S(1)} %slice_bitcast_fusion.1), channel_id=1, source_target_pairs={{0,1},{1,2},{2,3},{3,4},{4,5},{5,6},{6,7},{7,8},{8,9},{9,10},{10,1... | collective-permute-start | bytes 737288 | tf_op jit(solution)/shard_map/ppermute | solution.py:33
  15.0 12.1 %collective-permute-start.1 = (f32[5,96,128]{2,1,0:T(8,128)S(1)}, f32[5,96,128]{2,1,0:T(8,128)S(1)}, u32[]{:S(2)}, u32[]{:S(2)}) collective-permute-start(f32[5,96,128]{2,1,0:T(8,128)S(1)} %get-tuple-element.8), channel_id=1, source_target_pairs={{1,0},{2,1},{3,2},{4,3},{5,4},{6,5},{7,6},{8,7},{9,8},{10,9},{11,1... | collective-permute-start | bytes 737288 | tf_op jit(solution)/shard_map/ppermute | solution.py:34
  75.1 15.5 %collective-permute-start.2 = (f32[4,96,128]{2,1,0:T(8,128)S(1)}, f32[4,96,128]{2,1,0:T(8,128)S(1)}, u32[]{:S(2)}, u32[]{:S(2)}) collective-permute-start(f32[4,96,128]{2,1,0:T(8,128)S(1)} %get-tuple-element.6), channel_id=1, source_target_pairs={{0,1},{1,2},{2,3},{3,4},{4,5},{5,6},{6,7},{7,8},{8,9},{9,10},{10,1... | collective-permute-start | bytes 589832 | tf_op jit(solution)/shard_map/ppermute | solution.py:33
  87.4 11.2 %collective-permute-start.3 = (f32[4,96,128]{2,1,0:T(8,128)S(1)}, f32[4,96,128]{2,1,0:T(8,128)S(1)}, u32[]{:S(2)}, u32[]{:S(2)}) collective-permute-start(f32[4,96,128]{2,1,0:T(8,128)S(1)} %get-tuple-element.7), channel_id=1, source_target_pairs={{1,0},{2,1},{3,2},{4,3},{5,4},{6,5},{7,6},{8,7},{9,8},{10,9},{11,1... | collective-permute-start | bytes 589832 | tf_op jit(solution)/shard_map/ppermute | solution.py:34

commit v5 on v4

--- a/solution.py
+++ b/solution.py
@@ -77,8 +77,135 @@
     return (before + sx + after) / 9.0
 
 
-def drive_kernel(pair_ref, stack_ref, out_ref, mean_ref, spread_ref):
-    groups = stack_ref.shape[0]
+def pair_terms(g, pair_ref, stack_ref, mean_ref, spread_ref):
+    own = stack_ref[g]
+    mean_own = mean_ref[g]
+    spread_own = spread_ref[g]
+    center_own = own[1:-1] - mean_own
+    guarded_spread = jnp.maximum(spread_own, floor_variance)
+    drive_sum = None
+    for pairing_row in range(PAIRINGS):
+        h = pair_ref[pairing_row, g]
+        partner = stack_ref[h]
+        mean_partner = mean_ref[h]
+        spread_partner = spread_ref[h]
+        cross_term = box_rows(own * partner) - mean_own * mean_partner
+        factor = 2.0 * cross_term / jnp.maximum(spread_own * spread_partner, floor_product)
+        ratio_term = cross_term / guarded_spread
+        pair_term = factor * (partner[1:-1] - mean_partner - ratio_term * center_own)
+        drive_sum = pair_term if drive_sum is None else drive_sum + pair_term
+    return drive_sum
+
+
+def row_groups(first, count, rows):
+    groups = []
+    for r in range(first, first + count):
+        owner = r // rows
+        if groups and groups[-1][0] == owner:
+            groups[-1][2] += 1
+        else:
+            groups.append([owner, r - owner * rows, 1, r - first])
+    return groups
+
+
+def front_kernel(
+    pair_ref, own_ref, drive_ref, stack_ref, mean_ref, spread_ref, out_ref, zero_ref,
+    send_a, recv_a, send_h, recv_h, send_b, recv_b, send_c, recv_c, local_sem,
+):
+    mesh = pl.DeviceIdType.MESH
+    groups, width, y_rows, z_rows = stack_ref.shape
+    rows = width - 2
+    x_rows = own_ref.shape[0]
+    spaces = lax.axis_size("space")
+    me = lax.axis_index("img")
+    s = lax.axis_index("space")
+    has_lo = (s + spaces - 1) // spaces
+    has_hi = (2 * spaces - 2 - s) // spaces
+
+    barrier = pltpu.get_barrier_semaphore()
+    for offset in (-1, 0, 1):
+        exists = {-1: s > 0, 0: s >= 0, 1: s < spaces - 1}[offset]
+        for g in range(groups):
+            @pl.when(exists & ((offset != 0) | (me != g)))
+            def _():
+                pl.semaphore_signal(barrier, inc=1, device_id=(g, (s + offset + spaces) % spaces), device_id_type=mesh)
+    pl.semaphore_wait(barrier, groups * (1 + has_lo + has_hi) - 1)
+
+    zero_ref[...] = jnp.zeros(zero_ref.shape, jnp.float32)
+
+    def piece(t):
+        lo = max(t * rows - 1, 0)
+        hi = min(t * rows + rows + 1, x_rows)
+        return own_ref.at[pl.ds(lo, hi - lo)], lo - (t * rows - 1), hi - lo
+
+    def piece_copy(t, src_image):
+        src, dst_lo, count = piece(t)
+        dst = stack_ref.at[src_image, pl.ds(dst_lo, count)]
+        return src, dst
+
+    for t in range(groups):
+        src, dst = piece_copy(t, me)
+
+        @pl.when(me == t)
+        def _():
+            pltpu.make_async_copy(src, dst, local_sem.at[0]).start()
+
+        @pl.when(me != t)
+        def _():
+            pltpu.make_async_remote_copy(
+                src, dst, send_a.at[t], recv_a.at[me], device_id=(t, s), device_id_type=mesh
+            ).start()
+
+    @pl.when(s < spaces - 1)
+    def _():
+        pltpu.make_async_remote_copy(
+            own_ref.at[pl.ds(x_rows - 1, 1)], stack_ref.at[me, pl.ds(0, 1)],
+            send_h.at[0], recv_h.at[0, me], device_id=(0, (s + 1) % spaces), device_id_type=mesh,
+        ).start()
+
+    @pl.when(s > 0)
+    def _():
+        pltpu.make_async_remote_copy(
+            own_ref.at[pl.ds(0, 1)], stack_ref.at[me, pl.ds(width - 1, 1)],
+            send_h.at[1], recv_h.at[1, me], device_id=(groups - 1, (s + spaces - 1) % spaces), device_id_type=mesh,
+        ).start()
+
+    for t in range(groups):
+        src, dst = piece_copy(t, 0)
+        for g in range(groups):
+            @pl.when((me == t) & (me != g))
+            def _():
+                pltpu.make_async_remote_copy(
+                    src, stack_ref.at[g, pl.ds(piece(t)[1], piece(t)[2])],
+                    send_a.at[0], recv_a.at[g], device_id=(g, s), device_id_type=mesh,
+                ).wait_recv()
+
+        @pl.when(me == t)
+        def _():
+            pltpu.make_async_copy(src, dst, local_sem.at[0]).wait()
+
+    for g in range(groups):
+        @pl.when((me == 0) & (s > 0))
+        def _():
+            pltpu.make_async_remote_copy(
+                own_ref.at[pl.ds(0, 1)], stack_ref.at[g, pl.ds(0, 1)],
+                send_h.at[0], recv_h.at[0, g], device_id=(0, s), device_id_type=mesh,
+            ).wait_recv()
+
+        @pl.when((me == groups - 1) & (s < spaces - 1))
+        def _():
+            pltpu.make_async_remote_copy(
+                own_ref.at[pl.ds(0, 1)], stack_ref.at[g, pl.ds(width - 1, 1)],
+                send_h.at[1], recv_h.at[1, g], device_id=(0, s), device_id_type=mesh,
+            ).wait_recv()
+
+    @pl.when((me == 0) & (s == 0))
+    def _():
+        stack_ref[:, 0] = jnp.zeros((groups, y_rows, z_rows), jnp.float32)
+
+    @pl.when((me == groups - 1) & (s == spaces - 1))
+    def _():
+        stack_ref[:, width - 1] = jnp.zeros((groups, y_rows, z_rows), jnp.float32)
 
     def stats(g, carry):
         value = stack_ref[g]
@@ -89,59 +216,162 @@
 
     lax.fori_loop(0, groups, stats, 0)
 
+    below = row_groups(x_rows - RADIUS, RADIUS, rows)
+    above = row_groups(0, RADIUS, rows)
+
+    def main_copy(g):
+        src = out_ref.at[g]
+        dst = drive_ref.at[pl.ds(RADIUS + me * rows, rows)]
+        return src, dst
+
+    def halo_copies(g):
+        copies = []
+        for index, (owner, src_lo, count, dst_lo) in enumerate(below):
+            copies.append((owner, s < spaces - 1, 1, index, out_ref.at[g, pl.ds(src_lo, count)],
+                           drive_ref.at[pl.ds(dst_lo, count)]))
+        for index, (owner, src_lo, count, dst_lo) in enumerate(above):
+            copies.append((owner, s > 0, -1, len(below) + index, out_ref.at[g, pl.ds(src_lo, count)],
+                           drive_ref.at[pl.ds(x_rows + RADIUS + dst_lo, count)]))
+        return copies
+
     def pairs(g, carry):
-        own = stack_ref[g]
-        mean_own = mean_ref[g]
-        spread_own = spread_ref[g]
-        center_own = own[1:-1] - mean_own
-        guarded_spread = jnp.maximum(spread_own, floor_variance)
-        drive_sum = None
-        for pairing_row in range(PAIRINGS):
-            h = pair_ref[pairing_row, g]
-            partner = stack_ref[h]
-            mean_partner = mean_ref[h]
-            spread_partner = spread_ref[h]
-            cross_term = box_rows(own * partner) - mean_own * mean_partner
-            factor = 2.0 * cross_term / jnp.maximum(spread_own * spread_partner, floor_product)
-            ratio_term = cross_term / guarded_spread
-            pair_term = factor * (partner[1:-1] - mean_partner - ratio_term * center_own)
-            drive_sum = pair_term if drive_sum is None else drive_sum + pair_term
-        out_ref[g] = drive_sum
+        out_ref[g] = pair_terms(g, pair_ref, stack_ref, mean_ref, spread_ref)
+        src, dst = main_copy(g)
+
+        @pl.when(me == g)
+        def _():
+            pltpu.make_async_copy(src, dst, local_sem.at[1]).start()
+
+        @pl.when(me != g)
+        def _():
+            pltpu.make_async_remote_copy(
+                src, dst, send_b.at[g], recv_b.at[me], device_id=(g, s), device_id_type=mesh
+            ).start()
+
+        for owner, exists, offset, index, hsrc, hdst in halo_copies(g):
+            @pl.when((me == owner) & exists)
+            def _():
+                pltpu.make_async_remote_copy(
+                    hsrc, hdst, send_c.at[index, g], recv_c.at[index],
+                    device_id=(g, (s + offset + spaces) % spaces), device_id_type=mesh,
+                ).start()
         return carry
 
     lax.fori_loop(0, groups, pairs, 0)
 
-
-def slice_drive(stack, pairings):
-    groups, rows, y_rows, z_rows = stack.shape
-    shape = (groups, rows - 2, y_rows, z_rows)
+    @pl.when(s == 0)
+    def _():
+        pltpu.make_async_copy(zero_ref, drive_ref.at[pl.ds(0, RADIUS)], local_sem.at[2]).start()
+
+    @pl.when(s == spaces - 1)
+    def _():
+        pltpu.make_async_copy(
+            zero_ref, drive_ref.at[pl.ds(x_rows + RADIUS, RADIUS)], local_sem.at[3]
+        ).start()
+
+    for t in range(groups):
+        src, dst = piece_copy(t, me)
+
+        @pl.when(me != t)
+        def _():
+            pltpu.make_async_remote_copy(
+                src, dst, send_a.at[t], recv_a.at[me], device_id=(t, s), device_id_type=mesh
+            ).wait_send()
+
+    @pl.when(s < spaces - 1)
+    def _():
+        pltpu.make_async_remote_copy(
+            own_ref.at[pl.ds(x_rows - 1, 1)], stack_ref.at[me, pl.ds(0, 1)],
+            send_h.at[0], recv_h.at[0, me], device_id=(0, (s + 1) % spaces), device_id_type=mesh,
+        ).wait_send()
+
+    @pl.when(s > 0)
+    def _():
+        pltpu.make_async_remote_copy(
+            own_ref.at[pl.ds(0, 1)], stack_ref.at[me, pl.ds(width - 1, 1)],
+            send_h.at[1], recv_h.at[1, me], device_id=(groups - 1, (s + spaces - 1) % spaces), device_id_type=mesh,
+        ).wait_send()
+
+    for g in range(groups):
+        src, dst = main_copy(g)
+
+        @pl.when(me == g)
+        def _():
+            pltpu.make_async_copy(src, dst, local_sem.at[1]).wait()
+
+        @pl.when(me != g)
+        def _():
+            pltpu.make_async_remote_copy(
+                src, dst, send_b.at[g], recv_b.at[me], device_id=(g, s), device_id_type=mesh
+            ).wait_send()
+
+        for owner, exists, offset, index, hsrc, hdst in halo_copies(g):
+            @pl.when((me == owner) & exists)
+            def _():
+                pltpu.make_async_remote_copy(
+                    hsrc, hdst, send_c.at[index, g], recv_c.at[index],
+                    device_id=(g, (s + offset + spaces) % spaces), device_id_type=mesh,
+                ).wait_send()
+
+    for t in range(groups):
+        @pl.when(me != t)
+        def _():
+            pltpu.make_async_remote_copy(
+                out_ref.at[0], drive_ref.at[pl.ds(RADIUS + t * rows, rows)],
+                send_b.at[0], recv_b.at[t], device_id=(t, s), device_id_type=mesh,
+            ).wait_recv()
+
+    for owner, exists, offset, index, hsrc, hdst in halo_copies(0):
+        @pl.when(((offset == 1) & (s > 0)) | ((offset == -1) & (s < spaces - 1)))
+        def _():
+            pltpu.make_async_remote_copy(
+                hsrc, hdst, send_c.at[index, 0], recv_c.at[index],
+                device_id=(owner, s), device_id_type=mesh,
+            ).wait_recv()
+
+    @pl.when(s == 0)
+    def _():
+        pltpu.make_async_copy(zero_ref, drive_ref.at[pl.ds(0, RADIUS)], local_sem.at[2]).wait()
+
+    @pl.when(s == spaces - 1)
+    def _():
+        pltpu.make_async_copy(
+            zero_ref, drive_ref.at[pl.ds(x_rows + RADIUS, RADIUS)], local_sem.at[3]
+        ).wait()
+
+
+def front_stage(own, pairings, groups):
+    x_rows, y_rows, z_rows = own.shape
+    rows = x_rows // groups
+    shape = (groups, rows, y_rows, z_rows)
+    halos = len(row_groups(x_rows - RADIUS, RADIUS, rows)) + len(row_groups(0, RADIUS, rows))
+    dma = pltpu.SemaphoreType.DMA
     return pl.pallas_call(
-        drive_kernel,
-        out_shape=jax.ShapeDtypeStruct(shape, jnp.float32),
+        front_kernel,
+        out_shape=jax.ShapeDtypeStruct((x_rows + 2 * RADIUS, y_rows, z_rows), jnp.float32),
         in_specs=[
             pl.BlockSpec(memory_space=pltpu.SMEM),
             pl.BlockSpec(memory_space=pltpu.VMEM),
         ],
-        out_specs=pl.BlockSpec(memory_space=pltpu.VMEM),
-        scratch_shapes=[pltpu.VMEM(shape, jnp.float32), pltpu.VMEM(shape, jnp.float32)],
-    )(pairings, stack)
-
-
-def advect_rows(near_own, velocity):
-    center = near_own[1:-1]
-    backward = center - near_own[:-2]
-    forward = near_own[2:] - center
-    change = jnp.maximum(velocity[0], 0.0) * backward + jnp.minimum(velocity[0], 0.0) * forward
-    for dimension in range(1, 3):
-        length = center.shape[dimension]
-        padded = padded_along(center, dimension, 1)
-        backward = center - window(padded, dimension, 0, length)
-        forward = window(padded, dimension, 2, length) - center
-        speed_part = velocity[dimension]
-        change = change + (
-            jnp.maximum(speed_part, 0.0) * backward + jnp.minimum(speed_part, 0.0) * forward
-        )
-    return center - change
+        out_specs=pl.BlockSpec(memory_space=pl.ANY),
+        scratch_shapes=[
+            pltpu.VMEM((groups, rows + 2, y_rows, z_rows), jnp.float32),
+            pltpu.VMEM(shape, jnp.float32),
+            pltpu.VMEM(shape, jnp.float32),
+            pltpu.VMEM(shape, jnp.float32),
+            pltpu.VMEM((RADIUS, y_rows, z_rows), jnp.float32),
+            dma((groups,)),
+            dma((groups,)),
+            dma((2,)),
+            dma((2, groups)),
+            dma((groups,)),
+            dma((groups,)),
+            dma((halos, groups)),
+            dma((halos,)),
+            dma((4,)),
+        ],
+        compiler_params=pltpu.CompilerParams(collective_id=0, has_side_effects=True),
+    )(pairings, own)
 
 
 def shifted(value, offset, axis):
@@ -256,15 +486,8 @@
     groups = lax.axis_size("img")
     own = images[0]
     x_rows, y_rows, _ = own.shape
-    rows = x_rows // groups
     own_ext = halo_rows(own, RADIUS + 1)
-    near = own_ext[RADIUS:-RADIUS]
-    pieces = jnp.stack([near[j * rows:j * rows + rows + 2] for j in range(groups)])
-    stack = lax.all_to_all(pieces, "img", split_axis=0, concat_axis=0, tiled=True)
-    drive_part = slice_drive(stack, pairings)
-    returned = lax.all_to_all(drive_part, "img", split_axis=0, concat_axis=0, tiled=True)
-    drive_sum = returned.reshape(own.shape)
-    drive_ext = halo_rows(drive_sum, RADIUS)
+    drive_ext = front_stage(own, pairings, groups)
     velocity, advected = post_stage(drive_ext, own_ext)
     return (advected[None], velocity[None])
 

time: 119 us -> 96.8 us (0.81)
  the two profiles are of different devices: /device:TPU:69 before, /device:TPU:62 now
where the time goes in v5:
time: 96.8 us; the launch traced here: 96.6 us
  Pallas kernels  84.4 us (87%)
  starting transfers between devices  8.94 us (9%)
  other arithmetic  1.3 us (1%)
  local copies, waits for them, and re-layouts  1.2 us (1%)
    pallas_call x1, Pallas kernels, front_stage(): pl.pallas_call(front_kernel, out_shape=jax.ShapeDtypeStruct((x_rows + 2 *...  65.3 us
    pallas_call x1, Pallas kernels, post_stage(): pl.pallas_call(post_kernel, out_shape=(jax.ShapeDtypeStruct((3, x_rows, y...  19.2 us
    ppermute x1, starting transfers between devices, halo_rows(): after = lax.ppermute(value[:width], 'space', down)  7.01 us
  transfers between devices with their start and end apart: 2, of which 0 were waited for; matrix products, arithmetic and copies ran while one was open for 0% of the time, Pallas kernels for 68%

profile of v5, /device:TPU:62, one launch (start us, length us, event | category | flops | bytes accessed | tf_op | source)
XLA Modules:
  0.0 96.6 jit_solution(2961413253179671629)
XLA Ops:
  0.6 0.0 copy-start
  0.6 1.2 %slice_bitcast_fusion.1 = (f32[5,96,128]{2,1,0:T(8,128)S(1)}, f32[5,96,128]{2,1,0:T(8,128)S(1)}) fusion(f32[1,24,96,128]{3,2,1,0:T(8,128)} %param.3), kind=kLoop, calls=%fused_computation.2 | loop fusion | bytes 983040 | tf_op jit(solution)/shard_map/slice | solution.py:33
  1.8 1.9 %collective-permute-start = (f32[5,96,128]{2,1,0:T(8,128)S(1)}, f32[5,96,128]{2,1,0:T(8,128)S(1)}, u32[]{:S(2)}, u32[]{:S(2)}) collective-permute-start(f32[5,96,128]{2,1,0:T(8,128)S(1)} %get-tuple-element.6), channel_id=1, source_target_pairs={{0,1},{1,2},{2,3},{3,4},{4,5},{5,6},{6,7},{7,8},{8,9},{9,10},{10,1... | collective-permute-start | bytes 737288 | tf_op jit(solution)/shard_map/ppermute | solution.py:33
  3.8 7.0 %collective-permute-start.1 = (f32[5,96,128]{2,1,0:T(8,128)S(1)}, f32[5,96,128]{2,1,0:T(8,128)S(1)}, u32[]{:S(2)}, u32[]{:S(2)}) collective-permute-start(f32[5,96,128]{2,1,0:T(8,128)S(1)} %get-tuple-element.7), channel_id=1, source_target_pairs={{1,0},{2,1},{3,2},{4,3},{5,4},{6,5},{7,6},{8,7},{9,8},{10,9},{11,1... | collective-permute-start | bytes 737288 | tf_op jit(solution)/shard_map/ppermute | solution.py:34
  10.8 65.3 %shard_map.50.drive_ref = f32[32,96,128]{2,1,0:T(8,128)} custom-call(s32[3,8]{1,0:T(4,128)} %pair_ref.1, f32[24,96,128]{2,1,0:T(8,128)} %bitcast.7), custom_call_target="tpu_custom_call" | custom-call | tf_op jit(solution)/shard_map/pallas_call | solution.py:349
  76.1 0.0 collective-permute-done
  76.1 0.0 collective-permute-done.1
  76.1 0.0 copy-done
  76.1 1.3 %pad_maximum_fusion.own_ref = f32[34,96,128]{2,1,0:T(8,128)} fusion(f32[5,96,128]{2,1,0:T(8,128)S(1)} %collective-permute-done.1, f32[24,96,128]{2,1,0:T(8,128)S(1)} %bitcast.8, f32[5,96,128]{2,1,0:T(8,128)S(1)} %collective-permute-done), kind=kLoop, calls=%fused_computation | loop fusion | flops 835584 | bytes 3342336 | tf_op jit(solution)/shard_map/concatenate | solution.py:35
  77.4 19.2 %shard_map.51 = (f32[3,24,96,128]{3,2,1,0:T(8,128)}, f32[24,96,128]{2,1,0:T(8,128)}) custom-call(f32[32,96,128]{2,1,0:T(8,128)} %shard_map.50.drive_ref, f32[34,96,128]{2,1,0:T(8,128)} %pad_maximum_fusion.own_ref, f32[128,128]{1,0:T(8,128)} %constant.2.clone.wz_ref), custom_call_target="tpu_custom_call" | custom-call | tf_op jit(solution)/shard_map/pallas_call | solution.py:469
Async XLA Ops:
  0.6 75.5 %copy-start = (f32[1,24,96,128]{3,2,1,0:T(8,128)S(1)}, f32[1,24,96,128]{3,2,1,0:T(8,128)}, u32[]{:S(2)}) copy-start(f32[1,24,96,128]{3,2,1,0:T(8,128)} %param.3) | copy-start | bytes 3538948
  1.8 74.3 %collective-permute-start = (f32[5,96,128]{2,1,0:T(8,128)S(1)}, f32[5,96,128]{2,1,0:T(8,128)S(1)}, u32[]{:S(2)}, u32[]{:S(2)}) collective-permute-start(f32[5,96,128]{2,1,0:T(8,128)S(1)} %get-tuple-element.6), channel_id=1, source_target_pairs={{0,1},{1,2},{2,3},{3,4},{4,5},{5,6},{6,7},{7,8},{8,9},{9,10},{10,1... | collective-permute-start | bytes 737288 | tf_op jit(solution)/shard_map/ppermute | solution.py:33
  3.8 72.3 %collective-permute-start.1 = (f32[5,96,128]{2,1,0:T(8,128)S(1)}, f32[5,96,128]{2,1,0:T(8,128)S(1)}, u32[]{:S(2)}, u32[]{:S(2)}) collective-permute-start(f32[5,96,128]{2,1,0:T(8,128)S(1)} %get-tuple-element.7), channel_id=1, source_target_pairs={{1,0},{2,1},{3,2},{4,3},{5,4},{6,5},{7,6},{8,7},{9,8},{10,9},{11,1... | collective-permute-start | bytes 737288 | tf_op jit(solution)/shard_map/ppermute | solution.py:34

commit v6 on v5

--- a/solution.py
+++ b/solution.py
@@ -143,6 +143,27 @@
         dst = stack_ref.at[src_image, pl.ds(dst_lo, count)]
         return src, dst
 
+    def forward_copy(t_dyn, wait):
+        for kind in range(3):
+            cond = {0: t_dyn == 0, 1: t_dyn == groups - 1, 2: (t_dyn > 0) & (t_dyn < groups - 1)}[kind]
+
+            @pl.when(cond & (t_dyn != me))
+            def _():
+                if kind == 0:
+                    src, dst_lo, count = own_ref.at[pl.ds(0, rows + 1)], 1, rows + 1
+                elif kind == 1:
+                    src, dst_lo, count = own_ref.at[pl.ds(x_rows - rows - 1, rows + 1)], 0, rows + 1
+                else:
+                    src, dst_lo, count = own_ref.at[pl.ds(t_dyn * rows - 1, rows + 2)], 0, rows + 2
+                copy = pltpu.make_async_remote_copy(
+                    src, stack_ref.at[me, pl.ds(dst_lo, count)], send_a.at[t_dyn], recv_a.at[me],
+                    device_id=(t_dyn, s), device_id_type=mesh,
+                )
+                if wait:
+                    copy.wait_send()
+                else:
+                    copy.start()
+
     for t in range(groups):
         src, dst = piece_copy(t, me)
 
@@ -150,11 +171,8 @@
         def _():
             pltpu.make_async_copy(src, dst, local_sem.at[0]).start()
 
-        @pl.when(me != t)
-        def _():
-            pltpu.make_async_remote_copy(
-                src, dst, send_a.at[t], recv_a.at[me], device_id=(t, s), device_id_type=mesh
-            ).start()
+    for i in range(1, groups):
+        forward_copy((me + i) % groups, False)
 
     @pl.when(s < spaces - 1)
     def _():
@@ -170,21 +188,44 @@
             send_h.at[1], recv_h.at[1, me], device_id=(groups - 1, (s + spaces - 1) % spaces), device_id_type=mesh,
         ).start()
 
-    for t in range(groups):
-        src, dst = piece_copy(t, 0)
-        for g in range(groups):
-            @pl.when((me == t) & (me != g))
-            def _():
-                pltpu.make_async_remote_copy(
-                    src, stack_ref.at[g, pl.ds(piece(t)[1], piece(t)[2])],
-                    send_a.at[0], recv_a.at[g], device_id=(g, s), device_id_type=mesh,
-                ).wait_recv()
-
-        @pl.when(me == t)
-        def _():
-            pltpu.make_async_copy(src, dst, local_sem.at[0]).wait()
-
-    for g in range(groups):
+    def stats(g):
+        value = stack_ref[g]
+        mean = box_rows(value)
+        mean_ref[g] = mean
+        spread_ref[g] = box_rows(value * value) - mean * mean
+
+    @pl.when((me == 0) & (s == 0))
+    def _():
+        stack_ref[:, 0] = jnp.zeros((groups, y_rows, z_rows), jnp.float32)
+
+    @pl.when((me == groups - 1) & (s == spaces - 1))
+    def _():
+        stack_ref[:, width - 1] = jnp.zeros((groups, y_rows, z_rows), jnp.float32)
+
+    def arrive(i, carry):
+        g = (me + groups - i) % groups
+
+        @pl.when(i == 0)
+        def _():
+            for t in range(groups):
+                src, dst = piece_copy(t, me)
+
+                @pl.when(me == t)
+                def _():
+                    pltpu.make_async_copy(src, dst, local_sem.at[0]).wait()
+
+        @pl.when(i != 0)
+        def _():
+            for t in range(groups):
+                src, dst = piece_copy(t, 0)
+
+                @pl.when(me == t)
+                def _():
+                    pltpu.make_async_remote_copy(
+                        src, stack_ref.at[g, pl.ds(piece(t)[1], piece(t)[2])],
+                        send_a.at[0], recv_a.at[g], device_id=(g, s), device_id_type=mesh,
+                    ).wait_recv()
+
         @pl.when((me == 0) & (s > 0))
         def _():
             pltpu.make_async_remote_copy(
@@ -199,22 +240,10 @@
                 send_h.at[1], recv_h.at[1, g], device_id=(0, s), device_id_type=mesh,
             ).wait_recv()
 
-    @pl.when((me == 0) & (s == 0))
-    def _():
-        stack_ref[:, 0] = jnp.zeros((groups, y_rows, z_rows), jnp.float32)
-
-    @pl.when((me == groups - 1) & (s == spaces - 1))
-    def _():
-        stack_ref[:, width - 1] = jnp.zeros((groups, y_rows, z_rows), jnp.float32)
-
-    def stats(g, carry):
-        value = stack_ref[g]
-        mean = box_rows(value)
-        mean_ref[g] = mean
-        spread_ref[g] = box_rows(value * value) - mean * mean
+        stats(g)
         return carry
 
-    lax.fori_loop(0, groups, stats, 0)
+    lax.fori_loop(0, groups, arrive, 0)
 
     below = row_groups(x_rows - RADIUS, RADIUS, rows)
     above = row_groups(0, RADIUS, rows)
@@ -234,7 +263,8 @@
                            drive_ref.at[pl.ds(x_rows + RADIUS + dst_lo, count)]))
         return copies
 
-    def pairs(g, carry):
+    def pairs(i, carry):
+        g = (me + i) % groups
         out_ref[g] = pair_terms(g, pair_ref, stack_ref, mean_ref, spread_ref)
         src, dst = main_copy(g)
 
@@ -269,14 +299,8 @@
             zero_ref, drive_ref.at[pl.ds(x_rows + RADIUS, RADIUS)], local_sem.at[3]
         ).start()
 
-    for t in range(groups):
-        src, dst = piece_copy(t, me)
-
-        @pl.when(me != t)
-        def _():
-            pltpu.make_async_remote_copy(
-                src, dst, send_a.at[t], recv_a.at[me], device_id=(t, s), device_id_type=mesh
-            ).wait_send()
+    for i in range(1, groups):
+        forward_copy((me + i) % groups, True)
 
     @pl.when(s < spaces - 1)
     def _():

time: 96.8 us -> 96.5 us (level)
  no operation moved by 1% of the time
where the time goes in v6:
time: 96.5 us; the launch traced here: 96.3 us
  Pallas kernels  84.2 us (87%)
  starting transfers between devices  8.94 us (9%)
  other arithmetic  1.3 us (1%)
  local copies, waits for them, and re-layouts  1.2 us (1%)
    pallas_call x1, Pallas kernels, front_stage(): pl.pallas_call(front_kernel, out_shape=jax.ShapeDtypeStruct((x_rows + 2 *...  65.1 us
    pallas_call x1, Pallas kernels, post_stage(): pl.pallas_call(post_kernel, out_shape=(jax.ShapeDtypeStruct((3, x_rows, y...  19.1 us
    ppermute x1, starting transfers between devices, halo_rows(): after = lax.ppermute(value[:width], 'space', down)  7.01 us
  transfers between devices with their start and end apart: 2, of which 0 were waited for; matrix products, arithmetic and copies ran while one was open for 0% of the time, Pallas kernels for 68%

profile of v6, /device:TPU:62, one launch (start us, length us, event | category | flops | bytes accessed | tf_op | source)
XLA Modules:
  0.0 96.3 jit_solution(4416522361111278322)
XLA Ops:
  0.6 0.0 copy-start
  0.6 1.2 %slice_bitcast_fusion.1 = (f32[5,96,128]{2,1,0:T(8,128)S(1)}, f32[5,96,128]{2,1,0:T(8,128)S(1)}) fusion(f32[1,24,96,128]{3,2,1,0:T(8,128)} %param.3), kind=kLoop, calls=%fused_computation.2 | loop fusion | bytes 983040 | tf_op jit(solution)/shard_map/slice | solution.py:33
  1.8 1.9 %collective-permute-start = (f32[5,96,128]{2,1,0:T(8,128)S(1)}, f32[5,96,128]{2,1,0:T(8,128)S(1)}, u32[]{:S(2)}, u32[]{:S(2)}) collective-permute-start(f32[5,96,128]{2,1,0:T(8,128)S(1)} %get-tuple-element.6), channel_id=1, source_target_pairs={{0,1},{1,2},{2,3},{3,4},{4,5},{5,6},{6,7},{7,8},{8,9},{9,10},{10,1... | collective-permute-start | bytes 737288 | tf_op jit(solution)/shard_map/ppermute | solution.py:33
  3.8 7.0 %collective-permute-start.1 = (f32[5,96,128]{2,1,0:T(8,128)S(1)}, f32[5,96,128]{2,1,0:T(8,128)S(1)}, u32[]{:S(2)}, u32[]{:S(2)}) collective-permute-start(f32[5,96,128]{2,1,0:T(8,128)S(1)} %get-tuple-element.7), channel_id=1, source_target_pairs={{1,0},{2,1},{3,2},{4,3},{5,4},{6,5},{7,6},{8,7},{9,8},{10,9},{11,1... | collective-permute-start | bytes 737288 | tf_op jit(solution)/shard_map/ppermute | solution.py:34
  10.8 65.1 %shard_map.50.drive_ref = f32[32,96,128]{2,1,0:T(8,128)} custom-call(s32[3,8]{1,0:T(4,128)} %pair_ref.1, f32[24,96,128]{2,1,0:T(8,128)} %bitcast.7), custom_call_target="tpu_custom_call" | custom-call | tf_op jit(solution)/shard_map/pallas_call | solution.py:373
  75.9 0.0 collective-permute-done
  75.9 0.0 collective-permute-done.1
  75.9 0.0 copy-done
  75.9 1.3 %pad_maximum_fusion.own_ref = f32[34,96,128]{2,1,0:T(8,128)} fusion(f32[5,96,128]{2,1,0:T(8,128)S(1)} %collective-permute-done.1, f32[24,96,128]{2,1,0:T(8,128)S(1)} %bitcast.8, f32[5,96,128]{2,1,0:T(8,128)S(1)} %collective-permute-done), kind=kLoop, calls=%fused_computation | loop fusion | flops 835584 | bytes 3342336 | tf_op jit(solution)/shard_map/concatenate | solution.py:35
  77.2 19.1 %shard_map.51 = (f32[3,24,96,128]{3,2,1,0:T(8,128)}, f32[24,96,128]{2,1,0:T(8,128)}) custom-call(f32[32,96,128]{2,1,0:T(8,128)} %shard_map.50.drive_ref, f32[34,96,128]{2,1,0:T(8,128)} %pad_maximum_fusion.own_ref, f32[128,128]{1,0:T(8,128)} %constant.2.clone.wz_ref), custom_call_target="tpu_custom_call" | custom-call | tf_op jit(solution)/shard_map/pallas_call | solution.py:493
Async XLA Ops:
  0.6 75.3 %copy-start = (f32[1,24,96,128]{3,2,1,0:T(8,128)S(1)}, f32[1,24,96,128]{3,2,1,0:T(8,128)}, u32[]{:S(2)}) copy-start(f32[1,24,96,128]{3,2,1,0:T(8,128)} %param.3) | copy-start | bytes 3538948
  1.8 74.0 %collective-permute-start = (f32[5,96,128]{2,1,0:T(8,128)S(1)}, f32[5,96,128]{2,1,0:T(8,128)S(1)}, u32[]{:S(2)}, u32[]{:S(2)}) collective-permute-start(f32[5,96,128]{2,1,0:T(8,128)S(1)} %get-tuple-element.6), channel_id=1, source_target_pairs={{0,1},{1,2},{2,3},{3,4},{4,5},{5,6},{6,7},{7,8},{8,9},{9,10},{10,1... | collective-permute-start | bytes 737288 | tf_op jit(solution)/shard_map/ppermute | solution.py:33
  3.8 72.1 %collective-permute-start.1 = (f32[5,96,128]{2,1,0:T(8,128)S(1)}, f32[5,96,128]{2,1,0:T(8,128)S(1)}, u32[]{:S(2)}, u32[]{:S(2)}) collective-permute-start(f32[5,96,128]{2,1,0:T(8,128)S(1)} %get-tuple-element.7), channel_id=1, source_target_pairs={{1,0},{2,1},{3,2},{4,3},{5,4},{6,5},{7,6},{8,7},{9,8},{10,9},{11,1... | collective-permute-start | bytes 737288 | tf_op jit(solution)/shard_map/ppermute | solution.py:34

commit v7 on v6

--- a/solution.py
+++ b/solution.py
@@ -405,20 +405,36 @@
     return jnp.where((index >= 0) & (index < length), rolled, 0.0)
 
 
-def post_kernel(drive_ref, own_ref, wz_ref, vel_ref, adv_ref, force_ref, pass_ref):
-    extended, y_rows, _ = drive_ref.shape
+PAD = 8
+
+
+def post_kernel(drive_ref, own_ref, wz_ref, vel_ref, adv_ref, own_pad, force_ref, pass_ref):
+    extended, y_rows, z_rows = drive_ref.shape
     x_rows = vel_ref.shape[1]
+    padded = y_rows + 2 * PAD
     taps = gauss_taps(RADIUS)
+    zeros = jnp.zeros((PAD, z_rows), jnp.float32)
+
+    def inner(r, offset=0):
+        return (r, pl.ds(PAD + offset, y_rows))
+
+    def fill(r, carry):
+        own_pad[r, pl.ds(0, PAD)] = zeros
+        own_pad[r, pl.ds(PAD + y_rows, PAD)] = zeros
+        own_pad[inner(r)] = own_ref[r]
+        return carry
+
+    lax.fori_loop(0, own_ref.shape[0], fill, 0)
 
     def plane(c, r, count):
         return pl.ds(pl.multiple_of((c * count + r) * y_rows, 8), y_rows)
 
     def force_row(r, carry):
-        value = own_ref[r + 1]
+        value = own_pad[inner(r + 1)]
         drive = drive_ref[r]
-        force_ref[plane(0, r, extended)] = drive * ((own_ref[r + 2] - own_ref[r]) * 0.5)
+        force_ref[plane(0, r, extended)] = drive * ((own_pad[inner(r + 2)] - own_pad[inner(r)]) * 0.5)
         force_ref[plane(1, r, extended)] = drive * (
-            (shifted(value, 1, 0) - shifted(value, -1, 0)) * 0.5
+            (own_pad[inner(r + 1, 1)] - own_pad[inner(r + 1, -1)]) * 0.5
         )
         force_ref[plane(2, r, extended)] = drive * (
             (shifted(value, 1, 1) - shifted(value, -1, 1)) * 0.5
@@ -426,18 +442,24 @@
         return carry
 
     lax.fori_loop(0, extended, force_row, 0)
+
+    def slot(c, x):
+        return pl.multiple_of((c * x_rows + x) * padded, 8)
 
     def x_pass(x, carry):
         for c in range(3):
             acc = taps[0] * force_ref[plane(c, x, extended)]
             for t in range(1, len(taps)):
                 acc = acc + taps[t] * force_ref[plane(c, x + t, extended)]
-            pass_ref[plane(c, x, x_rows)] = acc
+            base = slot(c, x)
+            pass_ref[pl.ds(base, PAD)] = zeros
+            pass_ref[pl.ds(base + PAD, y_rows)] = acc
+            pass_ref[pl.ds(base + PAD + y_rows, PAD)] = zeros
         return carry
 
     lax.fori_loop(0, x_rows, x_pass, 0)
     wz = wz_ref[...]
-    chunk = 8 * y_rows
+    chunk = 8 * padded
     chunks = pass_ref.shape[0] // chunk
 
     def z_pass(i, carry):
@@ -451,21 +473,25 @@
     lax.fori_loop(0, chunks, z_pass, 0)
 
     def out_row(x, carry):
-        value = own_ref[x + RADIUS + 1]
+        r = x + RADIUS + 1
+        value = own_pad[inner(r)]
         change = None
         for c in range(3):
-            smoothed_z = pass_ref[plane(c, x, x_rows)]
-            acc = taps[0] * shifted(smoothed_z, -RADIUS, 0)
+            base = slot(c, x) + PAD - RADIUS
+            acc = taps[0] * pass_ref[pl.ds(base, y_rows)]
             for t in range(1, len(taps)):
-                acc = acc + taps[t] * shifted(smoothed_z, t - RADIUS, 0)
+                acc = acc + taps[t] * pass_ref[pl.ds(base + t, y_rows)]
             speed = step_scale * acc
             vel_ref[c, x] = speed
             if c == 0:
-                backward = value - own_ref[x + RADIUS]
-                forward = own_ref[x + RADIUS + 2] - value
+                backward = value - own_pad[inner(r - 1)]
+                forward = own_pad[inner(r + 1)] - value
+            elif c == 1:
+                backward = value - own_pad[inner(r, -1)]
+                forward = own_pad[inner(r, 1)] - value
             else:
-                backward = value - shifted(value, -1, c - 1)
-                forward = shifted(value, 1, c - 1) - value
+                backward = value - shifted(value, -1, 1)
+                forward = shifted(value, 1, 1) - value
             part = jnp.maximum(speed, 0.0) * backward + jnp.minimum(speed, 0.0) * forward
             change = part if change is None else change + part
         adv_ref[x] = value - change
@@ -499,8 +525,9 @@
         in_specs=[vmem] * 3,
         out_specs=(vmem, vmem),
         scratch_shapes=[
+            pltpu.VMEM((extended + 2, y_rows + 2 * PAD, z_rows), jnp.float32),
             pltpu.VMEM((3 * extended * y_rows, z_rows), jnp.float32),
-            pltpu.VMEM((3 * x_rows * y_rows, z_rows), jnp.float32),
+            pltpu.VMEM((3 * x_rows * (y_rows + 2 * PAD), z_rows), jnp.float32),
         ],
     )(drive_ext, own_ext, wz)
 

time: 96.5 us -> 95.3 us (0.988)
  Pallas kernels: 84.2 us -> 82.9 us
    pallas_call x1, Pallas kernels: 19.1 us -> 17.9 us  [post_stage(): pl.pallas_call(post_kernel, out_shape=(jax.ShapeDtypeStruct((3, x_rows, y...]
where the time goes in v7:
time: 95.3 us; the launch traced here: 95.1 us
  Pallas kernels  82.9 us (87%)
  starting transfers between devices  8.94 us (9%)
  other arithmetic  1.3 us (1%)
  local copies, waits for them, and re-layouts  1.2 us (1%)
    pallas_call x1, Pallas kernels, front_stage(): pl.pallas_call(front_kernel, out_shape=jax.ShapeDtypeStruct((x_rows + 2 *...  65.1 us
    pallas_call x1, Pallas kernels, post_stage(): pl.pallas_call(post_kernel, out_shape=(jax.ShapeDtypeStruct((3, x_rows, y...  17.9 us
    ppermute x1, starting transfers between devices, halo_rows(): after = lax.ppermute(value[:width], 'space', down)  7.01 us
    ppermute x1, starting transfers between devices, halo_rows(): before = lax.ppermute(value[-width:], 'space', up)  1.92 us
  transfers between devices with their start and end apart: 2, of which 0 were waited for; matrix products, arithmetic and copies ran while one was open for 0% of the time, Pallas kernels for 68%

profile of v7, /device:TPU:62, one launch (start us, length us, event | category | flops | bytes accessed | tf_op | source)
XLA Modules:
  0.0 95.1 jit_solution(3046328722589251567)
XLA Ops:
  0.6 0.0 copy-start
  0.6 1.2 %slice_bitcast_fusion.1 = (f32[5,96,128]{2,1,0:T(8,128)S(1)}, f32[5,96,128]{2,1,0:T(8,128)S(1)}) fusion(f32[1,24,96,128]{3,2,1,0:T(8,128)} %param.3), kind=kLoop, calls=%fused_computation.2 | loop fusion | bytes 983040 | tf_op jit(solution)/shard_map/slice | solution.py:33
  1.8 1.9 %collective-permute-start = (f32[5,96,128]{2,1,0:T(8,128)S(1)}, f32[5,96,128]{2,1,0:T(8,128)S(1)}, u32[]{:S(2)}, u32[]{:S(2)}) collective-permute-start(f32[5,96,128]{2,1,0:T(8,128)S(1)} %get-tuple-element.6), channel_id=1, source_target_pairs={{0,1},{1,2},{2,3},{3,4},{4,5},{5,6},{6,7},{7,8},{8,9},{9,10},{10,1... | collective-permute-start | bytes 737288 | tf_op jit(solution)/shard_map/ppermute | solution.py:33
  3.8 7.0 %collective-permute-start.1 = (f32[5,96,128]{2,1,0:T(8,128)S(1)}, f32[5,96,128]{2,1,0:T(8,128)S(1)}, u32[]{:S(2)}, u32[]{:S(2)}) collective-permute-start(f32[5,96,128]{2,1,0:T(8,128)S(1)} %get-tuple-element.7), channel_id=1, source_target_pairs={{1,0},{2,1},{3,2},{4,3},{5,4},{6,5},{7,6},{8,7},{9,8},{10,9},{11,1... | collective-permute-start | bytes 737288 | tf_op jit(solution)/shard_map/ppermute | solution.py:34
  10.8 65.1 %shard_map.50.drive_ref = f32[32,96,128]{2,1,0:T(8,128)} custom-call(s32[3,8]{1,0:T(4,128)} %pair_ref.1, f32[24,96,128]{2,1,0:T(8,128)} %bitcast.7), custom_call_target="tpu_custom_call" | custom-call | tf_op jit(solution)/shard_map/pallas_call | solution.py:373
  75.9 0.0 collective-permute-done
  75.9 0.0 collective-permute-done.1
  75.9 0.0 copy-done
  75.9 1.3 %pad_maximum_fusion.own_ref = f32[34,96,128]{2,1,0:T(8,128)} fusion(f32[5,96,128]{2,1,0:T(8,128)S(1)} %collective-permute-done.1, f32[24,96,128]{2,1,0:T(8,128)S(1)} %bitcast.8, f32[5,96,128]{2,1,0:T(8,128)S(1)} %collective-permute-done), kind=kLoop, calls=%fused_computation | loop fusion | flops 835584 | bytes 3342336 | tf_op jit(solution)/shard_map/concatenate | solution.py:35
  77.2 17.9 %shard_map.51 = (f32[3,24,96,128]{3,2,1,0:T(8,128)}, f32[24,96,128]{2,1,0:T(8,128)}) custom-call(f32[32,96,128]{2,1,0:T(8,128)} %shard_map.50.drive_ref, f32[34,96,128]{2,1,0:T(8,128)} %pad_maximum_fusion.own_ref, f32[128,128]{1,0:T(8,128)} %constant.2.clone.wz_ref), custom_call_target="tpu_custom_call" | custom-call | tf_op jit(solution)/shard_map/pallas_call | solution.py:519
Async XLA Ops:
  0.6 75.3 %copy-start = (f32[1,24,96,128]{3,2,1,0:T(8,128)S(1)}, f32[1,24,96,128]{3,2,1,0:T(8,128)}, u32[]{:S(2)}) copy-start(f32[1,24,96,128]{3,2,1,0:T(8,128)} %param.3) | copy-start | bytes 3538948
  1.8 74.0 %collective-permute-start = (f32[5,96,128]{2,1,0:T(8,128)S(1)}, f32[5,96,128]{2,1,0:T(8,128)S(1)}, u32[]{:S(2)}, u32[]{:S(2)}) collective-permute-start(f32[5,96,128]{2,1,0:T(8,128)S(1)} %get-tuple-element.6), channel_id=1, source_target_pairs={{0,1},{1,2},{2,3},{3,4},{4,5},{5,6},{6,7},{7,8},{8,9},{9,10},{10,1... | collective-permute-start | bytes 737288 | tf_op jit(solution)/shard_map/ppermute | solution.py:33
  3.8 72.1 %collective-permute-start.1 = (f32[5,96,128]{2,1,0:T(8,128)S(1)}, f32[5,96,128]{2,1,0:T(8,128)S(1)}, u32[]{:S(2)}, u32[]{:S(2)}) collective-permute-start(f32[5,96,128]{2,1,0:T(8,128)S(1)} %get-tuple-element.7), channel_id=1, source_target_pairs={{1,0},{2,1},{3,2},{4,3},{5,4},{6,5},{7,6},{8,7},{9,8},{10,9},{11,1... | collective-permute-start | bytes 737288 | tf_op jit(solution)/shard_map/ppermute | solution.py:34

commit v8 on v7

--- a/solution.py
+++ b/solution.py
@@ -465,7 +465,7 @@
     def z_pass(i, carry):
         rows = pl.ds(pl.multiple_of(i * chunk, 8), chunk)
         pass_ref[rows] = jnp.dot(
-            pass_ref[rows], wz, precision=lax.Precision.HIGHEST,
+            pass_ref[rows], wz, precision=lax.Precision.HIGH,
             preferred_element_type=jnp.float32,
         )
         return carry

time: 95.3 us -> 93.6 us (0.982)
  Pallas kernels: 82.9 us -> 81.3 us
    pallas_call x1, Pallas kernels: 17.9 us -> 16.2 us  [post_stage(): pl.pallas_call(post_kernel, out_shape=(jax.ShapeDtypeStruct((3, x_rows, y...]
  transfers between devices with their start and end apart: 2 -> 2, of which waited for: 0 -> 0; matrix products, arithmetic and copies ran while one was open for 0% -> 0% of each run, Pallas kernels for 68% -> 70%
where the time goes in v8:
time: 93.6 us; the launch traced here: 93.4 us
  Pallas kernels  81.3 us (87%)
  starting transfers between devices  8.94 us (10%)
  other arithmetic  1.3 us (1%)
  local copies, waits for them, and re-layouts  1.2 us (1%)
    pallas_call x1, Pallas kernels, front_stage(): pl.pallas_call(front_kernel, out_shape=jax.ShapeDtypeStruct((x_rows + 2 *...  65.1 us
    pallas_call x1, Pallas kernels, post_stage(): pl.pallas_call(post_kernel, out_shape=(jax.ShapeDtypeStruct((3, x_rows, y...  16.2 us
    ppermute x1, starting transfers between devices, halo_rows(): after = lax.ppermute(value[:width], 'space', down)  7.01 us
    ppermute x1, starting transfers between devices, halo_rows(): before = lax.ppermute(value[-width:], 'space', up)  1.92 us
  transfers between devices with their start and end apart: 2, of which 0 were waited for; matrix products, arithmetic and copies ran while one was open for 0% of the time, Pallas kernels for 70%

profile of v8, /device:TPU:62, one launch (start us, length us, event | category | flops | bytes accessed | tf_op | source)
XLA Modules:
  0.0 93.4 jit_solution(9757191926531830089)
XLA Ops:
  0.6 0.0 copy-start
  0.6 1.2 %slice_bitcast_fusion.1 = (f32[5,96,128]{2,1,0:T(8,128)S(1)}, f32[5,96,128]{2,1,0:T(8,128)S(1)}) fusion(f32[1,24,96,128]{3,2,1,0:T(8,128)} %param.3), kind=kLoop, calls=%fused_computation.2 | loop fusion | bytes 983040 | tf_op jit(solution)/shard_map/slice | solution.py:33
  1.8 1.9 %collective-permute-start = (f32[5,96,128]{2,1,0:T(8,128)S(1)}, f32[5,96,128]{2,1,0:T(8,128)S(1)}, u32[]{:S(2)}, u32[]{:S(2)}) collective-permute-start(f32[5,96,128]{2,1,0:T(8,128)S(1)} %get-tuple-element.6), channel_id=1, source_target_pairs={{0,1},{1,2},{2,3},{3,4},{4,5},{5,6},{6,7},{7,8},{8,9},{9,10},{10,1... | collective-permute-start | bytes 737288 | tf_op jit(solution)/shard_map/ppermute | solution.py:33
  3.8 7.0 %collective-permute-start.1 = (f32[5,96,128]{2,1,0:T(8,128)S(1)}, f32[5,96,128]{2,1,0:T(8,128)S(1)}, u32[]{:S(2)}, u32[]{:S(2)}) collective-permute-start(f32[5,96,128]{2,1,0:T(8,128)S(1)} %get-tuple-element.7), channel_id=1, source_target_pairs={{1,0},{2,1},{3,2},{4,3},{5,4},{6,5},{7,6},{8,7},{9,8},{10,9},{11,1... | collective-permute-start | bytes 737288 | tf_op jit(solution)/shard_map/ppermute | solution.py:34
  10.8 65.1 %shard_map.50.drive_ref = f32[32,96,128]{2,1,0:T(8,128)} custom-call(s32[3,8]{1,0:T(4,128)} %pair_ref.1, f32[24,96,128]{2,1,0:T(8,128)} %bitcast.7), custom_call_target="tpu_custom_call" | custom-call | tf_op jit(solution)/shard_map/pallas_call | solution.py:373
  75.9 0.0 collective-permute-done
  75.9 0.0 collective-permute-done.1
  75.9 0.0 copy-done
  75.9 1.3 %pad_maximum_fusion.own_ref = f32[34,96,128]{2,1,0:T(8,128)} fusion(f32[5,96,128]{2,1,0:T(8,128)S(1)} %collective-permute-done.1, f32[24,96,128]{2,1,0:T(8,128)S(1)} %bitcast.8, f32[5,96,128]{2,1,0:T(8,128)S(1)} %collective-permute-done), kind=kLoop, calls=%fused_computation | loop fusion | flops 835584 | bytes 3342336 | tf_op jit(solution)/shard_map/concatenate | solution.py:35
  77.2 16.2 %shard_map.51 = (f32[3,24,96,128]{3,2,1,0:T(8,128)}, f32[24,96,128]{2,1,0:T(8,128)}) custom-call(f32[32,96,128]{2,1,0:T(8,128)} %shard_map.50.drive_ref, f32[34,96,128]{2,1,0:T(8,128)} %pad_maximum_fusion.own_ref, f32[128,128]{1,0:T(8,128)} %constant.2.clone.wz_ref), custom_call_target="tpu_custom_call" | custom-call | tf_op jit(solution)/shard_map/pallas_call | solution.py:519
Async XLA Ops:
  0.6 75.3 %copy-start = (f32[1,24,96,128]{3,2,1,0:T(8,128)S(1)}, f32[1,24,96,128]{3,2,1,0:T(8,128)}, u32[]{:S(2)}) copy-start(f32[1,24,96,128]{3,2,1,0:T(8,128)} %param.3) | copy-start | bytes 3538948
  1.8 74.0 %collective-permute-start = (f32[5,96,128]{2,1,0:T(8,128)S(1)}, f32[5,96,128]{2,1,0:T(8,128)S(1)}, u32[]{:S(2)}, u32[]{:S(2)}) collective-permute-start(f32[5,96,128]{2,1,0:T(8,128)S(1)} %get-tuple-element.6), channel_id=1, source_target_pairs={{0,1},{1,2},{2,3},{3,4},{4,5},{5,6},{6,7},{7,8},{8,9},{9,10},{10,1... | collective-permute-start | bytes 737288 | tf_op jit(solution)/shard_map/ppermute | solution.py:33
  3.8 72.1 %collective-permute-start.1 = (f32[5,96,128]{2,1,0:T(8,128)S(1)}, f32[5,96,128]{2,1,0:T(8,128)S(1)}, u32[]{:S(2)}, u32[]{:S(2)}) collective-permute-start(f32[5,96,128]{2,1,0:T(8,128)S(1)} %get-tuple-element.7), channel_id=1, source_target_pairs={{1,0},{2,1},{3,2},{4,3},{5,4},{6,5},{7,6},{8,7},{9,8},{10,9},{11,1... | collective-permute-start | bytes 737288 | tf_op jit(solution)/shard_map/ppermute | solution.py:34

commit v9 on v8

--- a/solution.py
+++ b/solution.py
@@ -109,8 +109,8 @@
 
 
 def front_kernel(
-    pair_ref, own_ref, drive_ref, stack_ref, mean_ref, spread_ref, out_ref, zero_ref,
-    send_a, recv_a, send_h, recv_h, send_b, recv_b, send_c, recv_c, local_sem,
+    pair_ref, own_ref, drive_ref, ext_ref, stack_ref, mean_ref, spread_ref, out_ref, zero_ref,
+    send_a, recv_a, send_h, recv_h, send_b, recv_b, send_c, recv_c, local_sem, send_o, recv_o,
 ):
     mesh = pl.DeviceIdType.MESH
     groups, width, y_rows, z_rows = stack_ref.shape
@@ -132,6 +132,41 @@
     pl.semaphore_wait(barrier, groups * (1 + has_lo + has_hi) - 1)
 
     zero_ref[...] = jnp.zeros(zero_ref.shape, jnp.float32)
+    margin = RADIUS + 1
+
+    def own_halo(wait):
+        copies = [
+            (s < spaces - 1, own_ref.at[pl.ds(x_rows - margin, margin)], ext_ref.at[pl.ds(0, margin)],
+             0, (s + 1) % spaces),
+            (s > 0, own_ref.at[pl.ds(0, margin)], ext_ref.at[pl.ds(x_rows + margin, margin)],
+             1, (s + spaces - 1) % spaces),
+        ]
+        for exists, src, dst, index, target in copies:
+            @pl.when(exists)
+            def _():
+                copy = pltpu.make_async_remote_copy(
+                    src, dst, send_o.at[index], recv_o.at[index],
+                    device_id=(me, target), device_id_type=mesh,
+                )
+                if wait:
+                    copy.wait_send()
+                else:
+                    copy.start()
+        local = [
+            (s >= 0, own_ref, ext_ref.at[pl.ds(margin, x_rows)], 2),
+            (s == 0, zero_ref, ext_ref.at[pl.ds(0, margin)], 3),
+            (s == spaces - 1, zero_ref, ext_ref.at[pl.ds(x_rows + margin, margin)], 4),
+        ]
+        for exists, src, dst, index in local:
+            @pl.when(exists)
+            def _():
+                copy = pltpu.make_async_copy(src, dst, local_sem.at[index])
+                if wait:
+                    copy.wait()
+                else:
+                    copy.start()
+
+    own_halo(False)
 
     def piece(t):
         lo = max(t * rows - 1, 0)
@@ -291,12 +326,12 @@
 
     @pl.when(s == 0)
     def _():
-        pltpu.make_async_copy(zero_ref, drive_ref.at[pl.ds(0, RADIUS)], local_sem.at[2]).start()
+        pltpu.make_async_copy(zero_ref.at[pl.ds(0, RADIUS)], drive_ref.at[pl.ds(0, RADIUS)], local_sem.at[5]).start()
 
     @pl.when(s == spaces - 1)
     def _():
         pltpu.make_async_copy(
-            zero_ref, drive_ref.at[pl.ds(x_rows + RADIUS, RADIUS)], local_sem.at[3]
+            zero_ref.at[pl.ds(0, RADIUS)], drive_ref.at[pl.ds(x_rows + RADIUS, RADIUS)], local_sem.at[6]
         ).start()
 
     for i in range(1, groups):
@@ -353,14 +388,26 @@
                 device_id=(owner, s), device_id_type=mesh,
             ).wait_recv()
 
+    own_halo(True)
+    for exists, dst, index in (
+        (s > 0, ext_ref.at[pl.ds(0, margin)], 0),
+        (s < spaces - 1, ext_ref.at[pl.ds(x_rows + margin, margin)], 1),
+    ):
+        @pl.when(exists)
+        def _():
+            pltpu.make_async_remote_copy(
+                own_ref.at[pl.ds(0, margin)], dst, send_o.at[index], recv_o.at[index],
+                device_id=(me, s), device_id_type=mesh,
+            ).wait_recv()
+
     @pl.when(s == 0)
     def _():
-        pltpu.make_async_copy(zero_ref, drive_ref.at[pl.ds(0, RADIUS)], local_sem.at[2]).wait()
+        pltpu.make_async_copy(zero_ref.at[pl.ds(0, RADIUS)], drive_ref.at[pl.ds(0, RADIUS)], local_sem.at[5]).wait()
 
     @pl.when(s == spaces - 1)
     def _():
         pltpu.make_async_copy(
-            zero_ref, drive_ref.at[pl.ds(x_rows + RADIUS, RADIUS)], local_sem.at[3]
+            zero_ref.at[pl.ds(0, RADIUS)], drive_ref.at[pl.ds(x_rows + RADIUS, RADIUS)], local_sem.at[6]
         ).wait()
 
 
@@ -372,18 +419,21 @@
     dma = pltpu.SemaphoreType.DMA
     return pl.pallas_call(
         front_kernel,
-        out_shape=jax.ShapeDtypeStruct((x_rows + 2 * RADIUS, y_rows, z_rows), jnp.float32),
+        out_shape=(
+            jax.ShapeDtypeStruct((x_rows + 2 * RADIUS, y_rows, z_rows), jnp.float32),
+            jax.ShapeDtypeStruct((x_rows + 2 * RADIUS + 2, y_rows, z_rows), jnp.float32),
+        ),
         in_specs=[
             pl.BlockSpec(memory_space=pltpu.SMEM),
             pl.BlockSpec(memory_space=pltpu.VMEM),
         ],
-        out_specs=pl.BlockSpec(memory_space=pl.ANY),
+        out_specs=(pl.BlockSpec(memory_space=pl.ANY), pl.BlockSpec(memory_space=pl.ANY)),
         scratch_shapes=[
             pltpu.VMEM((groups, rows + 2, y_rows, z_rows), jnp.float32),
             pltpu.VMEM(shape, jnp.float32),
             pltpu.VMEM(shape, jnp.float32),
             pltpu.VMEM(shape, jnp.float32),
-            pltpu.VMEM((RADIUS, y_rows, z_rows), jnp.float32),
+            pltpu.VMEM((RADIUS + 1, y_rows, z_rows), jnp.float32),
             dma((groups,)),
             dma((groups,)),
             dma((2,)),
@@ -392,7 +442,9 @@
             dma((groups,)),
             dma((halos, groups)),
             dma((halos,)),
-            dma((4,)),
+            dma((7,)),
+            dma((2,)),
+            dma((2,)),
         ],
         compiler_params=pltpu.CompilerParams(collective_id=0, has_side_effects=True),
     )(pairings, own)
@@ -537,8 +589,7 @@
     groups = lax.axis_size("img")
     own = images[0]
     x_rows, y_rows, _ = own.shape
-    own_ext = halo_rows(own, RADIUS + 1)
-    drive_ext = front_stage(own, pairings, groups)
+    drive_ext, own_ext = front_stage(own, pairings, groups)
     velocity, advected = post_stage(drive_ext, own_ext)
     return (advected[None], velocity[None])
 

time: 93.6 us -> 87 us (0.929)
  the two profiles are of different devices: /device:TPU:62 before, /device:TPU:29 now
where the time goes in v9:
time: 87 us; the launch traced here: 86.9 us
  Pallas kernels  86.3 us (99%)
    pallas_call x1, Pallas kernels, front_stage(): pl.pallas_call(front_kernel, out_shape=(jax.ShapeDtypeStruct((x_rows + 2...  70.1 us
    pallas_call x1, Pallas kernels, post_stage(): pl.pallas_call(post_kernel, out_shape=(jax.ShapeDtypeStruct((3, x_rows, y...  16.2 us

profile of v9, /device:TPU:29, one launch (start us, length us, event | category | flops | bytes accessed | tf_op | source)
XLA Modules:
  0.0 86.9 jit_solution(9817846477165414187)
XLA Ops:
  0.6 70.1 %shard_map.50 = (f32[32,96,128]{2,1,0:T(8,128)}, f32[34,96,128]{2,1,0:T(8,128)}) custom-call(s32[3,8]{1,0:T(4,128)} %pair_ref.1, f32[24,96,128]{2,1,0:T(8,128)} %bitcast.3), custom_call_target="tpu_custom_call" | custom-call | tf_op jit(solution)/shard_map/pallas_call | solution.py:420
  70.7 16.2 %shard_map.51 = (f32[3,24,96,128]{3,2,1,0:T(8,128)}, f32[24,96,128]{2,1,0:T(8,128)}) custom-call(f32[32,96,128]{2,1,0:T(8,128)} %get-tuple-element.6.drive_ref, f32[34,96,128]{2,1,0:T(8,128)} %get-tuple-element.7.own_ref, f32[128,128]{1,0:T(8,128)} %constant.2.clone.wz_ref), custom_call_target="tpu_custom_call" | custom-call | tf_op jit(solution)/shard_map/pallas_call | solution.py:571

commit v10 on v9

--- a/solution.py
+++ b/solution.py
@@ -500,9 +500,10 @@
 
     def x_pass(x, carry):
         for c in range(3):
-            acc = taps[0] * force_ref[plane(c, x, extended)]
-            for t in range(1, len(taps)):
-                acc = acc + taps[t] * force_ref[plane(c, x + t, extended)]
+            acc = taps[RADIUS] * force_ref[plane(c, x + RADIUS, extended)]
+            for t in range(RADIUS):
+                pair = force_ref[plane(c, x + t, extended)] + force_ref[plane(c, x + 2 * RADIUS - t, extended)]
+                acc = acc + taps[t] * pair
             base = slot(c, x)
             pass_ref[pl.ds(base, PAD)] = zeros
             pass_ref[pl.ds(base + PAD, y_rows)] = acc
@@ -530,9 +531,10 @@
         change = None
         for c in range(3):
             base = slot(c, x) + PAD - RADIUS
-            acc = taps[0] * pass_ref[pl.ds(base, y_rows)]
-            for t in range(1, len(taps)):
-                acc = acc + taps[t] * pass_ref[pl.ds(base + t, y_rows)]
+            acc = taps[RADIUS] * pass_ref[pl.ds(base + RADIUS, y_rows)]
+            for t in range(RADIUS):
+                pair = pass_ref[pl.ds(base + t, y_rows)] + pass_ref[pl.ds(base + 2 * RADIUS - t, y_rows)]
+                acc = acc + taps[t] * pair
             speed = step_scale * acc
             vel_ref[c, x] = speed
             if c == 0:

time: 87 us -> 86.1 us (0.990)
  Pallas kernels: 86.3 us -> 85.4 us
    pallas_call x1, Pallas kernels: 16.2 us -> 15.3 us  [post_stage(): pl.pallas_call(post_kernel, out_shape=(jax.ShapeDtypeStruct((3, x_rows, y...]
where the time goes in v10:
time: 86.1 us; the launch traced here: 86 us
  Pallas kernels  85.4 us (99%)
    pallas_call x1, Pallas kernels, front_stage(): pl.pallas_call(front_kernel, out_shape=(jax.ShapeDtypeStruct((x_rows + 2...  70.1 us
    pallas_call x1, Pallas kernels, post_stage(): pl.pallas_call(post_kernel, out_shape=(jax.ShapeDtypeStruct((3, x_rows, y...  15.3 us

profile of v10, /device:TPU:29, one launch (start us, length us, event | category | flops | bytes accessed | tf_op | source)
XLA Modules:
  0.0 86.0 jit_solution(13811205400947690495)
XLA Ops:
  0.6 70.1 %shard_map.50 = (f32[32,96,128]{2,1,0:T(8,128)}, f32[34,96,128]{2,1,0:T(8,128)}) custom-call(s32[3,8]{1,0:T(4,128)} %pair_ref.1, f32[24,96,128]{2,1,0:T(8,128)} %bitcast.3), custom_call_target="tpu_custom_call" | custom-call | tf_op jit(solution)/shard_map/pallas_call | solution.py:420
  70.7 15.3 %shard_map.51 = (f32[3,24,96,128]{3,2,1,0:T(8,128)}, f32[24,96,128]{2,1,0:T(8,128)}) custom-call(f32[32,96,128]{2,1,0:T(8,128)} %get-tuple-element.6.drive_ref, f32[34,96,128]{2,1,0:T(8,128)} %get-tuple-element.7.own_ref, f32[128,128]{1,0:T(8,128)} %constant.2.clone.wz_ref), custom_call_target="tpu_custom_call" | custom-call | tf_op jit(solution)/shard_map/pallas_call | solution.py:573

commit v11 on v10

--- a/solution.py
+++ b/solution.py
@@ -460,7 +460,9 @@
 PAD = 8
 
 
-def post_kernel(drive_ref, own_ref, wz_ref, vel_ref, adv_ref, own_pad, force_ref, pass_ref):
+def post_kernel(
+    drive_ref, own_ref, wz_ref, vel_ref, adv_ref, own_pad, force_ref, pass_ref, vel_buf, adv_buf, sems
+):
     extended, y_rows, z_rows = drive_ref.shape
     x_rows = vel_ref.shape[1]
     padded = y_rows + 2 * PAD
@@ -536,7 +538,7 @@
                 pair = pass_ref[pl.ds(base + t, y_rows)] + pass_ref[pl.ds(base + 2 * RADIUS - t, y_rows)]
                 acc = acc + taps[t] * pair
             speed = step_scale * acc
-            vel_ref[c, x] = speed
+            vel_buf[c, x] = speed
             if c == 0:
                 backward = value - own_pad[inner(r - 1)]
                 forward = own_pad[inner(r + 1)] - value
@@ -548,10 +550,15 @@
                 forward = shifted(value, 1, 1) - value
             part = jnp.maximum(speed, 0.0) * backward + jnp.minimum(speed, 0.0) * forward
             change = part if change is None else change + part
-        adv_ref[x] = value - change
+        adv_buf[x] = value - change
+        row = pl.ds(x, 1)
+        pltpu.make_async_copy(vel_buf.at[:, row], vel_ref.at[:, row], sems.at[0]).start()
+        pltpu.make_async_copy(adv_buf.at[row], adv_ref.at[row], sems.at[1]).start()
         return carry
 
     lax.fori_loop(0, x_rows, out_row, 0)
+    pltpu.make_async_copy(vel_buf, vel_ref, sems.at[0]).wait()
+    pltpu.make_async_copy(adv_buf, adv_ref, sems.at[1]).wait()
 
 
 def band(length, taps):
@@ -577,11 +584,14 @@
             jax.ShapeDtypeStruct((x_rows, y_rows, z_rows), jnp.float32),
         ),
         in_specs=[vmem] * 3,
-        out_specs=(vmem, vmem),
+        out_specs=(pl.BlockSpec(memory_space=pl.ANY), pl.BlockSpec(memory_space=pl.ANY)),
         scratch_shapes=[
             pltpu.VMEM((extended + 2, y_rows + 2 * PAD, z_rows), jnp.float32),
             pltpu.VMEM((3 * extended * y_rows, z_rows), jnp.float32),
             pltpu.VMEM((3 * x_rows * (y_rows + 2 * PAD), z_rows), jnp.float32),
+            pltpu.VMEM((3, x_rows, y_rows, z_rows), jnp.float32),
+            pltpu.VMEM((x_rows, y_rows, z_rows), jnp.float32),
+            pltpu.SemaphoreType.DMA((2,)),
         ],
     )(drive_ext, own_ext, wz)
 

time: 86.1 us -> 84.7 us (0.984)
  Pallas kernels: 85.4 us -> 83.9 us
    pallas_call x1, Pallas kernels: 15.3 us -> 13.8 us  [post_stage(): pl.pallas_call(post_kernel, out_shape=(jax.ShapeDtypeStruct((3, x_rows, y...]
where the time goes in v11:
time: 84.7 us; the launch traced here: 84.5 us
  Pallas kernels  83.9 us (99%)
    pallas_call x1, Pallas kernels, front_stage(): pl.pallas_call(front_kernel, out_shape=(jax.ShapeDtypeStruct((x_rows + 2...  70.1 us
    pallas_call x1, Pallas kernels, post_stage(): pl.pallas_call(post_kernel, out_shape=(jax.ShapeDtypeStruct((3, x_rows, y...  13.8 us

profile of v11, /device:TPU:29, one launch (start us, length us, event | category | flops | bytes accessed | tf_op | source)
XLA Modules:
  0.0 84.5 jit_solution(8100599540563583279)
XLA Ops:
  0.6 70.1 %shard_map.50 = (f32[32,96,128]{2,1,0:T(8,128)}, f32[34,96,128]{2,1,0:T(8,128)}) custom-call(s32[3,8]{1,0:T(4,128)} %pair_ref.1, f32[24,96,128]{2,1,0:T(8,128)} %bitcast.3), custom_call_target="tpu_custom_call" | custom-call | tf_op jit(solution)/shard_map/pallas_call | solution.py:420
  70.7 13.8 %shard_map.51 = (f32[3,24,96,128]{3,2,1,0:T(8,128)}, f32[24,96,128]{2,1,0:T(8,128)}) custom-call(f32[32,96,128]{2,1,0:T(8,128)} %get-tuple-element.6.drive_ref, f32[34,96,128]{2,1,0:T(8,128)} %get-tuple-element.7.own_ref, f32[128,128]{1,0:T(8,128)} %constant.2.clone.wz_ref), custom_call_target="tpu_custom_call" | custom-call | tf_op jit(solution)/shard_map/pallas_call | solution.py:580

commit v12 on v11

--- a/solution.py
+++ b/solution.py
@@ -461,7 +461,8 @@
 
 
 def post_kernel(
-    drive_ref, own_ref, wz_ref, vel_ref, adv_ref, own_pad, force_ref, pass_ref, vel_buf, adv_buf, sems
+    drive_hbm, own_ref, wz_ref, vel_ref, adv_ref, own_pad, force_ref, pass_ref, vel_buf, adv_buf, sems,
+    drive_ref, own_sems, drive_sems,
 ):
     extended, y_rows, z_rows = drive_ref.shape
     x_rows = vel_ref.shape[1]
@@ -472,18 +473,38 @@
     def inner(r, offset=0):
         return (r, pl.ds(PAD + offset, y_rows))
 
+    def own_copy(r):
+        return pltpu.make_async_copy(own_ref.at[r], own_pad.at[inner(r)], own_sems.at[r])
+
+    def drive_copy(r):
+        return pltpu.make_async_copy(drive_hbm.at[r], drive_ref.at[r], drive_sems.at[r])
+
+    def start(r, carry):
+        own_copy(r).start()
+        return carry
+
     def fill(r, carry):
         own_pad[r, pl.ds(0, PAD)] = zeros
         own_pad[r, pl.ds(PAD + y_rows, PAD)] = zeros
-        own_pad[inner(r)] = own_ref[r]
         return carry
 
     lax.fori_loop(0, own_ref.shape[0], fill, 0)
+    lax.fori_loop(0, own_ref.shape[0], start, 0)
+
+    def start_drive(r, carry):
+        drive_copy(r).start()
+        return carry
+
+    lax.fori_loop(0, extended, start_drive, 0)
+    own_copy(0).wait()
+    own_copy(1).wait()
 
     def plane(c, r, count):
         return pl.ds(pl.multiple_of((c * count + r) * y_rows, 8), y_rows)
 
     def force_row(r, carry):
+        own_copy(r + 2).wait()
+        drive_copy(r).wait()
         value = own_pad[inner(r + 1)]
         drive = drive_ref[r]
         force_ref[plane(0, r, extended)] = drive * ((own_pad[inner(r + 2)] - own_pad[inner(r)]) * 0.5)
@@ -583,7 +604,7 @@
             jax.ShapeDtypeStruct((3, x_rows, y_rows, z_rows), jnp.float32),
             jax.ShapeDtypeStruct((x_rows, y_rows, z_rows), jnp.float32),
         ),
-        in_specs=[vmem] * 3,
+        in_specs=[pl.BlockSpec(memory_space=pl.ANY), pl.BlockSpec(memory_space=pl.ANY), vmem],
         out_specs=(pl.BlockSpec(memory_space=pl.ANY), pl.BlockSpec(memory_space=pl.ANY)),
         scratch_shapes=[
             pltpu.VMEM((extended + 2, y_rows + 2 * PAD, z_rows), jnp.float32),
@@ -592,6 +613,9 @@
             pltpu.VMEM((3, x_rows, y_rows, z_rows), jnp.float32),
             pltpu.VMEM((x_rows, y_rows, z_rows), jnp.float32),
             pltpu.SemaphoreType.DMA((2,)),
+            pltpu.VMEM((extended, y_rows, z_rows), jnp.float32),
+            pltpu.SemaphoreType.DMA((extended + 2,)),
+            pltpu.SemaphoreType.DMA((extended,)),
         ],
     )(drive_ext, own_ext, wz)
 

time: 84.7 us -> 85.7 us (1.012)
  Pallas kernels: 83.9 us -> 84.9 us
    pallas_call x1, Pallas kernels: 13.8 us -> 14.8 us  [post_stage(): pl.pallas_call(post_kernel, out_shape=(jax.ShapeDtypeStruct((3, x_rows, y...]
where the time goes in v12:
time: 85.7 us; the launch traced here: 85.5 us
  Pallas kernels  84.9 us (99%)
    pallas_call x1, Pallas kernels, front_stage(): pl.pallas_call(front_kernel, out_shape=(jax.ShapeDtypeStruct((x_rows + 2...  70.1 us
    pallas_call x1, Pallas kernels, post_stage(): pl.pallas_call(post_kernel, out_shape=(jax.ShapeDtypeStruct((3, x_rows, y...  14.8 us

profile of v12, /device:TPU:29, one launch (start us, length us, event | category | flops | bytes accessed | tf_op | source)
XLA Modules:
  0.0 85.5 jit_solution(10341307385521410022)
XLA Ops:
  0.6 70.1 %shard_map.50 = (f32[32,96,128]{2,1,0:T(8,128)}, f32[34,96,128]{2,1,0:T(8,128)}) custom-call(s32[3,8]{1,0:T(4,128)} %pair_ref.1, f32[24,96,128]{2,1,0:T(8,128)} %bitcast.3), custom_call_target="tpu_custom_call" | custom-call | tf_op jit(solution)/shard_map/pallas_call | solution.py:420
  70.7 14.8 %shard_map.51 = (f32[3,24,96,128]{3,2,1,0:T(8,128)}, f32[24,96,128]{2,1,0:T(8,128)}) custom-call(f32[32,96,128]{2,1,0:T(8,128)} %get-tuple-element.6.drive_hbm, f32[34,96,128]{2,1,0:T(8,128)} %get-tuple-element.7.own_ref, f32[128,128]{1,0:T(8,128)} %constant.2.clone.wz_ref), custom_call_target="tpu_custom_call" | custom-call | tf_op jit(solution)/shard_map/pallas_call | solution.py:601

commit v13 on v11

--- a/solution.py
+++ b/solution.py
@@ -461,7 +461,8 @@
 
 
 def post_kernel(
-    drive_ref, own_ref, wz_ref, vel_ref, adv_ref, own_pad, force_ref, pass_ref, vel_buf, adv_buf, sems
+    drive_ref, own_ref, wz_ref, vel_ref, adv_ref, own_pad, force_ref, pass_ref, vel_buf, adv_buf, sems,
+    compact_ref,
 ):
     extended, y_rows, z_rows = drive_ref.shape
     x_rows = vel_ref.shape[1]
@@ -508,21 +509,25 @@
                 acc = acc + taps[t] * pair
             base = slot(c, x)
             pass_ref[pl.ds(base, PAD)] = zeros
-            pass_ref[pl.ds(base + PAD, y_rows)] = acc
             pass_ref[pl.ds(base + PAD + y_rows, PAD)] = zeros
+            compact_ref[plane(c, x, x_rows)] = acc
         return carry
 
     lax.fori_loop(0, x_rows, x_pass, 0)
     wz = wz_ref[...]
-    chunk = 8 * padded
-    chunks = pass_ref.shape[0] // chunk
+    per_chunk = 8
+    chunk = per_chunk * y_rows
+    chunks = compact_ref.shape[0] // chunk
 
     def z_pass(i, carry):
         rows = pl.ds(pl.multiple_of(i * chunk, 8), chunk)
-        pass_ref[rows] = jnp.dot(
-            pass_ref[rows], wz, precision=lax.Precision.HIGH,
+        result = jnp.dot(
+            compact_ref[rows], wz, precision=lax.Precision.HIGH,
             preferred_element_type=jnp.float32,
         )
+        for k in range(per_chunk):
+            base = pl.multiple_of((i * per_chunk + k) * padded + PAD, 8)
+            pass_ref[pl.ds(base, y_rows)] = result[k * y_rows:(k + 1) * y_rows]
         return carry
 
     lax.fori_loop(0, chunks, z_pass, 0)
@@ -592,6 +597,7 @@
             pltpu.VMEM((3, x_rows, y_rows, z_rows), jnp.float32),
             pltpu.VMEM((x_rows, y_rows, z_rows), jnp.float32),
             pltpu.SemaphoreType.DMA((2,)),
+            pltpu.VMEM((3 * x_rows * y_rows, z_rows), jnp.float32),
         ],
     )(drive_ext, own_ext, wz)
 

time: 84.7 us -> 84.4 us (level)
  no operation moved by 1% of the time
where the time goes in v13:
time: 84.4 us; the launch traced here: 84.3 us
  Pallas kernels  83.7 us (99%)
    pallas_call x1, Pallas kernels, front_stage(): pl.pallas_call(front_kernel, out_shape=(jax.ShapeDtypeStruct((x_rows + 2...  70.1 us
    pallas_call x1, Pallas kernels, post_stage(): pl.pallas_call(post_kernel, out_shape=(jax.ShapeDtypeStruct((3, x_rows, y...  13.6 us

profile of v13, /device:TPU:29, one launch (start us, length us, event | category | flops | bytes accessed | tf_op | source)
XLA Modules:
  0.0 84.3 jit_solution(6329604759113330328)
XLA Ops:
  0.6 70.1 %shard_map.50 = (f32[32,96,128]{2,1,0:T(8,128)}, f32[34,96,128]{2,1,0:T(8,128)}) custom-call(s32[3,8]{1,0:T(4,128)} %pair_ref.1, f32[24,96,128]{2,1,0:T(8,128)} %bitcast.3), custom_call_target="tpu_custom_call" | custom-call | tf_op jit(solution)/shard_map/pallas_call | solution.py:420
  70.7 13.6 %shard_map.51 = (f32[3,24,96,128]{3,2,1,0:T(8,128)}, f32[24,96,128]{2,1,0:T(8,128)}) custom-call(f32[32,96,128]{2,1,0:T(8,128)} %get-tuple-element.6.drive_ref, f32[34,96,128]{2,1,0:T(8,128)} %get-tuple-element.7.own_ref, f32[128,128]{1,0:T(8,128)} %constant.2.clone.wz_ref), custom_call_target="tpu_custom_call" | custom-call | tf_op jit(solution)/shard_map/pallas_call | solution.py:585

commit v14 on v13

--- a/solution.py
+++ b/solution.py
@@ -74,7 +74,7 @@
     row = lax.broadcasted_iota(jnp.int32, sx.shape, 1)
     before = jnp.where(row >= 1, pltpu.roll(sx, 1, 1), 0.0)
     after = jnp.where(row < last, pltpu.roll(sx, last, 1), 0.0)
-    return (before + sx + after) / 9.0
+    return (before + sx + after) * (1.0 / 9.0)
 
 
 def pair_terms(g, pair_ref, stack_ref, mean_ref, spread_ref):
@@ -82,7 +82,7 @@
     mean_own = mean_ref[g]
     spread_own = spread_ref[g]
     center_own = own[1:-1] - mean_own
-    guarded_spread = jnp.maximum(spread_own, floor_variance)
+    inverse_spread = 1.0 / jnp.maximum(spread_own, floor_variance)
     drive_sum = None
     for pairing_row in range(PAIRINGS):
         h = pair_ref[pairing_row, g]
@@ -91,7 +91,7 @@
         spread_partner = spread_ref[h]
         cross_term = box_rows(own * partner) - mean_own * mean_partner
         factor = 2.0 * cross_term / jnp.maximum(spread_own * spread_partner, floor_product)
-        ratio_term = cross_term / guarded_spread
+        ratio_term = cross_term * inverse_spread
         pair_term = factor * (partner[1:-1] - mean_partner - ratio_term * center_own)
         drive_sum = pair_term if drive_sum is None else drive_sum + pair_term
     return drive_sum

time: 84.4 us -> 84.4 us (level)
  no operation moved by 1% of the time
where the time goes in v14:
time: 84.4 us; the launch traced here: 84.3 us
  Pallas kernels  83.7 us (99%)
    pallas_call x1, Pallas kernels, front_stage(): pl.pallas_call(front_kernel, out_shape=(jax.ShapeDtypeStruct((x_rows + 2...  70.1 us
    pallas_call x1, Pallas kernels, post_stage(): pl.pallas_call(post_kernel, out_shape=(jax.ShapeDtypeStruct((3, x_rows, y...  13.6 us

profile of v14, /device:TPU:29, one launch (start us, length us, event | category | flops | bytes accessed | tf_op | source)
XLA Modules:
  0.0 84.3 jit_solution(3140102177619776021)
XLA Ops:
  0.6 70.1 %shard_map.50 = (f32[32,96,128]{2,1,0:T(8,128)}, f32[34,96,128]{2,1,0:T(8,128)}) custom-call(s32[3,8]{1,0:T(4,128)} %pair_ref.1, f32[24,96,128]{2,1,0:T(8,128)} %bitcast.3), custom_call_target="tpu_custom_call" | custom-call | tf_op jit(solution)/shard_map/pallas_call | solution.py:420
  70.7 13.6 %shard_map.51 = (f32[3,24,96,128]{3,2,1,0:T(8,128)}, f32[24,96,128]{2,1,0:T(8,128)}) custom-call(f32[32,96,128]{2,1,0:T(8,128)} %get-tuple-element.6.drive_ref, f32[34,96,128]{2,1,0:T(8,128)} %get-tuple-element.7.own_ref, f32[128,128]{1,0:T(8,128)} %constant.2.clone.wz_ref), custom_call_target="tpu_custom_call" | custom-call | tf_op jit(solution)/shard_map/pallas_call | solution.py:585

commit v15 on v14

--- a/solution.py
+++ b/solution.py
@@ -515,7 +515,7 @@
 
     lax.fori_loop(0, x_rows, x_pass, 0)
     wz = wz_ref[...]
-    per_chunk = 8
+    per_chunk = 24
     chunk = per_chunk * y_rows
     chunks = compact_ref.shape[0] // chunk
 

time: 84.4 us -> 83.5 us (0.989)
  Pallas kernels: 83.7 us -> 82.7 us
    pallas_call x1, Pallas kernels: 13.6 us -> 12.6 us  [post_stage(): pl.pallas_call(post_kernel, out_shape=(jax.ShapeDtypeStruct((3, x_rows, y...]
where the time goes in v15:
time: 83.5 us; the launch traced here: 83.4 us
  Pallas kernels  82.7 us (99%)
    pallas_call x1, Pallas kernels, front_stage(): pl.pallas_call(front_kernel, out_shape=(jax.ShapeDtypeStruct((x_rows + 2...  70.1 us
    pallas_call x1, Pallas kernels, post_stage(): pl.pallas_call(post_kernel, out_shape=(jax.ShapeDtypeStruct((3, x_rows, y...  12.6 us

profile of v15, /device:TPU:29, one launch (start us, length us, event | category | flops | bytes accessed | tf_op | source)
XLA Modules:
  0.0 83.4 jit_solution(1725316012076015716)
XLA Ops:
  0.6 70.1 %shard_map.50 = (f32[32,96,128]{2,1,0:T(8,128)}, f32[34,96,128]{2,1,0:T(8,128)}) custom-call(s32[3,8]{1,0:T(4,128)} %pair_ref.1, f32[24,96,128]{2,1,0:T(8,128)} %bitcast.3), custom_call_target="tpu_custom_call" | custom-call | tf_op jit(solution)/shard_map/pallas_call | solution.py:420
  70.7 12.6 %shard_map.51 = (f32[3,24,96,128]{3,2,1,0:T(8,128)}, f32[24,96,128]{2,1,0:T(8,128)}) custom-call(f32[32,96,128]{2,1,0:T(8,128)} %get-tuple-element.6.drive_ref, f32[34,96,128]{2,1,0:T(8,128)} %get-tuple-element.7.own_ref, f32[128,128]{1,0:T(8,128)} %constant.2.clone.wz_ref), custom_call_target="tpu_custom_call" | custom-call | tf_op jit(solution)/shard_map/pallas_call | solution.py:585

commit v16 on v15

--- a/solution.py
+++ b/solution.py
@@ -515,7 +515,7 @@
 
     lax.fori_loop(0, x_rows, x_pass, 0)
     wz = wz_ref[...]
-    per_chunk = 24
+    per_chunk = 72
     chunk = per_chunk * y_rows
     chunks = compact_ref.shape[0] // chunk
 

time: 83.5 us -> 83.2 us (level)
  no operation moved by 1% of the time
where the time goes in v16:
time: 83.2 us; the launch traced here: 83.1 us
  Pallas kernels  82.4 us (99%)
    pallas_call x1, Pallas kernels, front_stage(): pl.pallas_call(front_kernel, out_shape=(jax.ShapeDtypeStruct((x_rows + 2...  70.1 us
    pallas_call x1, Pallas kernels, post_stage(): pl.pallas_call(post_kernel, out_shape=(jax.ShapeDtypeStruct((3, x_rows, y...  12.3 us

profile of v16, /device:TPU:29, one launch (start us, length us, event | category | flops | bytes accessed | tf_op | source)
XLA Modules:
  0.0 83.1 jit_solution(5194142188158764818)
XLA Ops:
  0.6 70.1 %shard_map.50 = (f32[32,96,128]{2,1,0:T(8,128)}, f32[34,96,128]{2,1,0:T(8,128)}) custom-call(s32[3,8]{1,0:T(4,128)} %pair_ref.1, f32[24,96,128]{2,1,0:T(8,128)} %bitcast.3), custom_call_target="tpu_custom_call" | custom-call | tf_op jit(solution)/shard_map/pallas_call | solution.py:420
  70.7 12.3 %shard_map.51 = (f32[3,24,96,128]{3,2,1,0:T(8,128)}, f32[24,96,128]{2,1,0:T(8,128)}) custom-call(f32[32,96,128]{2,1,0:T(8,128)} %get-tuple-element.6.drive_ref, f32[34,96,128]{2,1,0:T(8,128)} %get-tuple-element.7.own_ref, f32[128,128]{1,0:T(8,128)} %constant.2.clone.wz_ref), custom_call_target="tpu_custom_call" | custom-call | tf_op jit(solution)/shard_map/pallas_call | solution.py:585

commit v17 on v16

--- a/solution.py
+++ b/solution.py
@@ -513,7 +513,7 @@
             compact_ref[plane(c, x, x_rows)] = acc
         return carry
 
-    lax.fori_loop(0, x_rows, x_pass, 0)
+    lax.fori_loop(0, x_rows, x_pass, 0, unroll=2)
     wz = wz_ref[...]
     per_chunk = 72
     chunk = per_chunk * y_rows
@@ -561,7 +561,7 @@
         pltpu.make_async_copy(adv_buf.at[row], adv_ref.at[row], sems.at[1]).start()
         return carry
 
-    lax.fori_loop(0, x_rows, out_row, 0)
+    lax.fori_loop(0, x_rows, out_row, 0, unroll=2)
     pltpu.make_async_copy(vel_buf, vel_ref, sems.at[0]).wait()
     pltpu.make_async_copy(adv_buf, adv_ref, sems.at[1]).wait()
 

time: 83.2 us -> 82.8 us (level)
  no operation moved by 1% of the time
where the time goes in v17:
time: 82.8 us; the launch traced here: 82.7 us
  Pallas kernels  82.1 us (99%)
    pallas_call x1, Pallas kernels, front_stage(): pl.pallas_call(front_kernel, out_shape=(jax.ShapeDtypeStruct((x_rows + 2...  70.1 us
    pallas_call x1, Pallas kernels, post_stage(): pl.pallas_call(post_kernel, out_shape=(jax.ShapeDtypeStruct((3, x_rows, y...  12 us

profile of v17, /device:TPU:29, one launch (start us, length us, event | category | flops | bytes accessed | tf_op | source)
XLA Modules:
  0.0 82.7 jit_solution(17367289474292291554)
XLA Ops:
  0.6 70.1 %shard_map.50 = (f32[32,96,128]{2,1,0:T(8,128)}, f32[34,96,128]{2,1,0:T(8,128)}) custom-call(s32[3,8]{1,0:T(4,128)} %pair_ref.1, f32[24,96,128]{2,1,0:T(8,128)} %bitcast.3), custom_call_target="tpu_custom_call" | custom-call | tf_op jit(solution)/shard_map/pallas_call | solution.py:420
  70.7 12.0 %shard_map.51 = (f32[3,24,96,128]{3,2,1,0:T(8,128)}, f32[24,96,128]{2,1,0:T(8,128)}) custom-call(f32[32,96,128]{2,1,0:T(8,128)} %get-tuple-element.6.drive_ref, f32[34,96,128]{2,1,0:T(8,128)} %get-tuple-element.7.own_ref, f32[128,128]{1,0:T(8,128)} %constant.2.clone.wz_ref), custom_call_target="tpu_custom_call" | custom-call | tf_op jit(solution)/shard_map/pallas_call | solution.py:585

commit v18 on v17

--- a/solution.py
+++ b/solution.py
@@ -496,7 +496,7 @@
         )
         return carry
 
-    lax.fori_loop(0, extended, force_row, 0)
+    lax.fori_loop(0, extended, force_row, 0, unroll=2)
 
     def slot(c, x):
         return pl.multiple_of((c * x_rows + x) * padded, 8)

time: 82.8 us -> 81.7 us (0.987)
  Pallas kernels: 82.1 us -> 80.9 us
    pallas_call x1, Pallas kernels: 12 us -> 10.8 us  [post_stage(): pl.pallas_call(post_kernel, out_shape=(jax.ShapeDtypeStruct((3, x_rows, y...]
where the time goes in v18:
time: 81.7 us; the launch traced here: 81.5 us
  Pallas kernels  80.9 us (99%)
    pallas_call x1, Pallas kernels, front_stage(): pl.pallas_call(front_kernel, out_shape=(jax.ShapeDtypeStruct((x_rows + 2...  70.1 us
    pallas_call x1, Pallas kernels, post_stage(): pl.pallas_call(post_kernel, out_shape=(jax.ShapeDtypeStruct((3, x_rows, y...  10.8 us

profile of v18, /device:TPU:29, one launch (start us, length us, event | category | flops | bytes accessed | tf_op | source)
XLA Modules:
  0.0 81.5 jit_solution(12314508613464063937)
XLA Ops:
  0.6 70.1 %shard_map.50 = (f32[32,96,128]{2,1,0:T(8,128)}, f32[34,96,128]{2,1,0:T(8,128)}) custom-call(s32[3,8]{1,0:T(4,128)} %pair_ref.1, f32[24,96,128]{2,1,0:T(8,128)} %bitcast.3), custom_call_target="tpu_custom_call" | custom-call | tf_op jit(solution)/shard_map/pallas_call | solution.py:420
  70.7 10.8 %shard_map.51 = (f32[3,24,96,128]{3,2,1,0:T(8,128)}, f32[24,96,128]{2,1,0:T(8,128)}) custom-call(f32[32,96,128]{2,1,0:T(8,128)} %get-tuple-element.6.drive_ref, f32[34,96,128]{2,1,0:T(8,128)} %get-tuple-element.7.own_ref, f32[128,128]{1,0:T(8,128)} %constant.2.clone.wz_ref), custom_call_target="tpu_custom_call" | custom-call | tf_op jit(solution)/shard_map/pallas_call | solution.py:585
